TPU v7x, 32 devices: a whole 2x2x4 slice. The times are simulated.
32 devices in a mesh: slab: 2 (over y), col: 4 (over x, core), row: 4 (over z).
Axes of the slice: x: 2, y: 2, z: 4, core: 2. Of those that a mesh axis runs over, the one named last changes fastest.
Arguments:
- tokens: bfloat16 [256, 256, 384], P(('slab', 'row'), 'col'), parts along dimension 0, may hold values from -6 to 6
- norm_gain: float32 [384], replicated, may hold values from 0.1 to 1.9
- query_weight: bfloat16 [384, 384], replicated, may hold values from -0.3125 to 0.3125
- key_weight: bfloat16 [384, 384], replicated, may hold values from -0.3125 to 0.3125
- value_weight: bfloat16 [384, 384], replicated, may hold values from -0.3125 to 0.3125
- out_weight: bfloat16 [384, 384], replicated, may hold values from -0.3125 to 0.3125
- head_scale: float32 [6], replicated, may hold values from 4 to 12
- counts: int32 [32, 16], P(('slab', 'row'), 'col'), parts along dimension 0, may hold values from 0 to 4, as said below
- sources: int32 [32, 16, 4], P(('slab', 'row'), 'col'), parts along dimension 0, may hold values from 0 to 255, as said below
Outputs:
- inpainted: bfloat16 [256, 256, 384], P(('slab', 'row'), 'col'), parts along dimension 0
There are 2 independent parts, one for each index of `slab`. A program takes and returns all parts, laid end to end along the dimension named above; an argument that names none is the same for every part. Nothing has to cross between parts.
Inputs may be any that keep to these rules, and one draw needn't show every extreme that they name: `counts`: each block of 4 x 4 tiles whose first tile row and column are multiples of 4 and 4 has at least the smaller of 4 and 8 and at most 8 tiles with a count above 0. `sources`: every entry names a tile of the same band of 4 tile rows as its own tile (the same tile row divided by 4). Entry j of tile t with j below counts[t] names a tile whose count is 0; the other entries are arbitrary tiles of that band. Among the entries below the counts of all tiles of one block of 4 x 4 tiles, at most 8 name tiles of any one block of 4 tile columns.
All inputs are finite; a program needn't handle non-finite values.
Results may differ from a plain program's by a relative error of at most 0.0041.
Values may be sent and summed in bfloat16 or wider, within the bound.
No kernel may reach another device: no remote copies, remote signals or barrier semaphores. Data moves between devices by JAX's collectives and lax.ppermute only.
A program may use at most 192 MiB of HBM per device.

v0:
```python
import jax
import jax.numpy as jnp
from jax import lax
from jax.sharding import PartitionSpec as P

HEADS = 6
TILE_ROWS = 8
TILE_COLS = 16
RADIUS = 3
S_MAX = 4
MASK_MOST = 8


def extended(block, sides, width):
    for axis, dim in sides:
        count = lax.axis_size(axis)
        forward = [(i, i + 1) for i in range(count - 1)]
        backward = [(target, source) for source, target in forward]
        low = lax.ppermute(
            lax.slice_in_dim(block, block.shape[dim] - width, None, axis=dim), axis, forward
        )
        high = lax.ppermute(lax.slice_in_dim(block, 0, width, axis=dim), axis, backward)
        block = jnp.concatenate([low, block, high], axis=dim)
    return block


def normalize(flat_tokens, norm_gain):
    as_float = flat_tokens.astype(jnp.float32)
    inverse_rms = lax.rsqrt(jnp.mean(as_float * as_float, axis=-1, keepdims=True) + 1e-06)
    return (as_float * inverse_rms * norm_gain).astype(jnp.bfloat16)


def unit_heads(projected, head_factor):
    split_heads = projected.reshape(projected.shape[0], head_factor.shape[0], -1)
    inverse_len = lax.rsqrt(jnp.sum(split_heads * split_heads, axis=-1, keepdims=True) + 1e-06)
    return (
        (split_heads * inverse_len * head_factor[:, None])
        .reshape(projected.shape)
        .astype(jnp.bfloat16)
    )


def keys_values(normed, key_weight, value_weight):
    unit_scale = jnp.ones((HEADS,), jnp.float32)
    key_rows = unit_heads(
        jnp.dot(normed, key_weight, preferred_element_type=jnp.float32), unit_scale
    )
    value_rows = jnp.dot(normed, value_weight, preferred_element_type=jnp.float32).astype(
        jnp.bfloat16
    )
    return (key_rows, value_rows)


def band_halves():
    win_rows = TILE_ROWS + 2 * RADIUS
    query_row = jnp.arange(TILE_ROWS, dtype=jnp.int32)[:, None, None, None]
    query_col = jnp.arange(TILE_COLS, dtype=jnp.int32)[None, :, None, None]
    key_row = jnp.arange(win_rows, dtype=jnp.int32)[None, None, :, None]
    key_col = jnp.arange(2 * TILE_COLS, dtype=jnp.int32)[None, None, None, :]
    inside = (
        (key_row >= query_row)
        & (key_row <= query_row + 2 * RADIUS)
        & (key_col >= query_col)
        & (key_col <= query_col + 2 * RADIUS)
    )
    return inside.astype(jnp.float32)


def pick_tiles(source_grid, offset, wanted, tile_cols):
    row_pick = (
        (wanted // tile_cols)[..., None, None] * TILE_ROWS
        + offset
        + jnp.arange(TILE_ROWS, dtype=jnp.int32)[:, None]
    )
    col_pick = (
        (wanted % tile_cols)[..., None, None] * TILE_COLS
        + offset
        + jnp.arange(TILE_COLS, dtype=jnp.int32)[None, :]
    )
    picked = source_grid[row_pick, col_pick]
    return picked.reshape(wanted.shape + (TILE_ROWS * TILE_COLS, source_grid.shape[-1]))


def body(
    tokens,
    norm_gain,
    query_weight,
    key_weight,
    value_weight,
    out_weight,
    head_scale,
    counts,
    sources,
):
    grid_rows, grid_cols, feature = tokens.shape
    tile_rows = grid_rows // TILE_ROWS
    tile_cols = grid_cols // TILE_COLS
    per_device = tile_rows * tile_cols
    tile_size = TILE_ROWS * TILE_COLS
    head_size = feature // HEADS
    win_rows = TILE_ROWS + 2 * RADIUS
    col_count = lax.axis_size("col")
    capacity = max(2, (MASK_MOST * S_MAX + col_count - 1) // col_count)
    slot_count = col_count * capacity
    flat_tokens = tokens.reshape(grid_rows * grid_cols, feature)
    normed = normalize(flat_tokens, norm_gain)
    query_unit = unit_heads(
        jnp.dot(normed, query_weight, preferred_element_type=jnp.float32), head_scale
    )
    valid_tiles = (counts == 0).astype(jnp.bfloat16)
    valid_cells = jnp.broadcast_to(
        valid_tiles[:, None, :, None], (tile_rows, TILE_ROWS, tile_cols, TILE_COLS)
    ).reshape(grid_rows, grid_cols)
    normed_grid = normed.reshape(grid_rows, grid_cols, feature)
    padded_rows = grid_rows + 2 * RADIUS
    padded_cols = grid_cols + 2 * RADIUS
    halo_normed, halo_valid = (
        extended(normed_grid, (("col", 1), ("row", 0)), RADIUS),
        extended(valid_cells, (("col", 1), ("row", 0)), RADIUS),
    )
    halo_keys, halo_values = keys_values(halo_normed.reshape(-1, feature), key_weight, value_weight)
    halo_keys = halo_keys.reshape(padded_rows, padded_cols, feature)
    halo_values = halo_values.reshape(padded_rows, padded_cols, feature)
    source_offset = RADIUS
    right_pad = TILE_COLS - 2 * RADIUS
    near_keys = jnp.pad(halo_keys, ((0, 0), (0, right_pad), (0, 0)))
    near_values = jnp.pad(halo_values, ((0, 0), (0, right_pad), (0, 0)))
    near_valid = jnp.pad(halo_valid.astype(jnp.float32), ((0, 0), (0, right_pad)))
    band_mask = band_halves()
    query_strips = query_unit.reshape(tile_rows, TILE_ROWS, tile_cols, TILE_COLS, HEADS, head_size)

    def near_row(row_index):
        key_strip = lax.dynamic_slice_in_dim(near_keys, row_index * TILE_ROWS, win_rows, 0).reshape(
            win_rows, tile_cols + 1, TILE_COLS, HEADS, head_size
        )
        value_strip = lax.dynamic_slice_in_dim(
            near_values, row_index * TILE_ROWS, win_rows, 0
        ).reshape(win_rows, tile_cols + 1, TILE_COLS, HEADS, head_size)
        valid_strip = lax.dynamic_slice_in_dim(
            near_valid, row_index * TILE_ROWS, win_rows, 0
        ).reshape(win_rows, tile_cols + 1, TILE_COLS)
        query_strip = lax.dynamic_index_in_dim(query_strips, row_index, 0, keepdims=False)
        weight_total = jnp.zeros((tile_cols, HEADS, TILE_ROWS, TILE_COLS), jnp.float32)
        summed = jnp.zeros((TILE_ROWS, tile_cols, TILE_COLS, HEADS, head_size), jnp.float32)
        for half in range(2):
            key_part = key_strip[:, half : half + tile_cols]
            value_part = value_strip[:, half : half + tile_cols]
            valid_part = valid_strip[:, half : half + tile_cols].transpose(1, 0, 2)
            band_part = band_mask[..., half * TILE_COLS : (half + 1) * TILE_COLS]
            scores = jnp.einsum(
                "rbchd,sbkhd->bhrcsk", query_strip, key_part, preferred_element_type=jnp.float32
            )
            weights = jnp.exp(scores) * band_part[None, None] * valid_part[:, None, None, None]
            weight_total = weight_total + jnp.sum(weights, axis=(4, 5))
            summed = summed + jnp.einsum(
                "bhrcsk,sbkhd->rbchd",
                weights.astype(jnp.bfloat16),
                value_part,
                preferred_element_type=jnp.float32,
            )
        weight_total = weight_total.transpose(2, 0, 3, 1).reshape(TILE_ROWS, grid_cols, HEADS)
        return (summed.reshape(TILE_ROWS, grid_cols, HEADS, head_size), weight_total)

    near_sum, near_total = lax.map(near_row, jnp.arange(tile_rows, dtype=jnp.int32))
    band_index = lax.axis_index("row")
    all_cols = tile_cols * col_count
    flat_counts = counts.reshape(per_device)
    flat_sources = sources.reshape(per_device * S_MAX)
    live_mask = (jnp.arange(S_MAX, dtype=jnp.int32)[None, :] < flat_counts[:, None]).reshape(-1)
    source_row = flat_sources // all_cols
    source_col = flat_sources % all_cols
    owner_col = source_col // tile_cols
    remote_tile = (source_row - band_index * tile_rows) * tile_cols + source_col % tile_cols
    owner_hits = (
        (owner_col[:, None] == jnp.arange(col_count, dtype=jnp.int32)[None, :]) & live_mask[:, None]
    ).astype(jnp.int32)
    owner_rank = jnp.sum((jnp.cumsum(owner_hits, axis=0) - owner_hits) * owner_hits, axis=1)
    slot_index = jnp.where(live_mask, owner_col * capacity + owner_rank, 0)
    slot_hits = (
        slot_index[:, None] == jnp.arange(slot_count, dtype=jnp.int32)[None, :]
    ) & live_mask[:, None]
    requests = jnp.sum(jnp.where(slot_hits, remote_tile[:, None], 0), axis=0).reshape(
        col_count, capacity
    )
    wanted = lax.all_to_all(requests, "col", split_axis=0, concat_axis=0, tiled=True)
    far_keys = lax.all_to_all(
        pick_tiles(halo_keys, source_offset, wanted, tile_cols),
        "col",
        split_axis=0,
        concat_axis=0,
        tiled=True,
    )
    far_values = lax.all_to_all(
        pick_tiles(halo_values, source_offset, wanted, tile_cols),
        "col",
        split_axis=0,
        concat_axis=0,
        tiled=True,
    )
    far_keys = far_keys.reshape(slot_count, tile_size, HEADS, head_size)
    far_values = far_values.reshape(slot_count, tile_size, HEADS, head_size)
    slot_owner = jnp.any(slot_hits.reshape(per_device, S_MAX, slot_count), axis=1).reshape(
        tile_rows, tile_cols, slot_count
    )
    query_grid = query_unit.reshape(tile_rows, TILE_ROWS, tile_cols, TILE_COLS, feature)
    slot_queries = jnp.einsum(
        "abs,arbcd->srcd",
        slot_owner.astype(jnp.bfloat16),
        query_grid,
        preferred_element_type=jnp.float32,
    ).astype(jnp.bfloat16)
    slot_queries = slot_queries.reshape(slot_count, tile_size, HEADS, head_size)
    far_scores = jnp.einsum(
        "sqhd,skhd->shqk", slot_queries, far_keys, preferred_element_type=jnp.float32
    )
    far_weights = jnp.exp(far_scores)
    slot_total = jnp.sum(far_weights, axis=-1)
    slot_sum = jnp.einsum(
        "shqk,skhd->sqhd",
        far_weights.astype(jnp.bfloat16),
        far_values,
        preferred_element_type=jnp.float32,
    )
    owner_float = slot_owner.astype(jnp.float32)
    far_sum = jnp.einsum(
        "abs,srchd->arbchd",
        owner_float,
        slot_sum.reshape(slot_count, TILE_ROWS, TILE_COLS, HEADS, head_size),
        precision=lax.Precision.HIGHEST,
    )
    far_total = jnp.einsum(
        "abs,shrc->arbch",
        owner_float,
        slot_total.reshape(slot_count, HEADS, TILE_ROWS, TILE_COLS),
        precision=lax.Precision.HIGHEST,
    )
    far_sum = far_sum.reshape(tile_rows, TILE_ROWS, grid_cols, HEADS, head_size)
    far_total = far_total.reshape(tile_rows, TILE_ROWS, grid_cols, HEADS)
    numerator = near_sum + far_sum
    denominator = near_total + far_total
    attended = (numerator / denominator[..., None]).astype(jnp.bfloat16).reshape(-1, feature)
    mixed_rows = flat_tokens.astype(jnp.float32) + jnp.dot(
        attended, out_weight, preferred_element_type=jnp.float32
    )
    return mixed_rows.astype(jnp.bfloat16).reshape(grid_rows, grid_cols, feature)


def solution(mesh):
    placed = (
        P(("slab", "row"), "col", None),
        P(),
        P(),
        P(),
        P(),
        P(),
        P(),
        P(("slab", "row"), "col"),
        P(("slab", "row"), "col", None),
    )
    return jax.shard_map(
        body, mesh=mesh, in_specs=placed, out_specs=P(("slab", "row"), "col", None), check_vma=False
    )
```

profile of v0, /device:TPU:8, one launch (start us, length us, event | category | flops | bytes accessed | tf_op | source)
XLA Modules:
  0.0 621.9 jit_solution(4314318006058874166)
XLA Ops:
  5.3 3.0 collective-permute-start
  10.5 4.2 collective-permute-start.4
  17.2 3.2 all-to-all-start
  20.7 2.8 multiply_reduce_fusion.1
  26.8 3.5 collective-permute-start.2
  30.5 2.7 collective-permute-done.3
  37.6 2.6 reshape.491
  41.8 4.9 convert_element_type.86
  46.7 6.1 copy.192
  52.8 44.7 %gather_fusion.1 = bf16[4096,384]{1,0:T(8,128)(2,1)} fusion(bf16[38,70,384]{2,1,0:T(8,128)(2,1)S(1)} %copy.192, s32[4096]{0:T(1024)S(1)} %reshape.469), kind=kCustom, calls=%fused_computation.1 | custom fusion | bytes 6324224 | tf_op jit(solution)/shard_map/gather | solution.py:80
  97.5 4.6 copy.158
  102.1 4.8 all-to-all-start.2
  107.0 3.5 multiply_convert_fusion.1
  110.7 5.6 copy.154
  116.3 6.1 convert_element_type.90
  122.5 4.5 bitcast_convert_fusion
  129.8 19.2 %collective-permute-start.6 = (bf16[3,70]{1,0:T(4,128)(2,1)S(1)}, bf16[3,70]{1,0:T(4,128)(2,1)S(1)}, u32[]{:S(2)}, u32[]{:S(2)}) collective-permute-start(bf16[3,70]{1,0:T(4,128)(2,1)S(1)} %get-tuple-element.164), channel_id=1, source_target_pairs={{0,1},{1,2},{2,3},{4,5},{5,6},{6,7},{8,9},{9,10},{10,11},{12,13},{... | collective-permute-start | bytes 1268 | tf_op jit(solution)/shard_map/ppermute | solution.py:19
  150.5 4.1 copy.145
  154.6 10.6 %reshape.498 = bf16[32,128,6,64]{3,2,0,1:T(8,128)(2,1)} reshape(bf16[32,8,16,384]{3,0,2,1:T(8,128)(2,1)} %bitcast_convert_fusion) | data formatting | bytes 6291456 | tf_op jit(solution)/shard_map/reshape | solution.py:212
  166.0 3.9 reshape.448
  169.9 4.5 convolution_convert_fusion
  174.4 3.9 reshape.449
  183.1 44.7 %gather_fusion = bf16[4096,384]{1,0:T(8,128)(2,1)} fusion(bf16[38,70,384]{2,1,0:T(8,128)(2,1)S(1)} %copy-done.3, s32[4096]{0:T(1024)S(1)} %reshape.469), kind=kCustom, calls=%fused_computation | custom fusion | bytes 6324224 | tf_op jit(solution)/shard_map/gather | solution.py:80
  227.9 4.7 copy.151
  232.5 4.6 all-to-all-start.1
  237.2 308.2 %while.13 = (s32[]{:T(128)}, f32[4,8,64,6,64]{4,2,3,1,0:T(8,128)}, f32[4,8,64,6]{2,1,3,0:T(8,128)S(1)}, s32[4]{0:T(128)S(1)}, bf16[38,80,384]{2,1,0:T(8,128)(2,1...) while((s32[]{:T(128)}, f32[4,8,64,6,64]{4,2,3,1,0:T(8,128)}, ...), condition=%wide.region_6.7_spmd.clone, body=%wide.region_3.6_spmd.clone.sunk | while | flops 360772608 | bytes 40591132 | solution.py:164
  240.3 2.5 constant_dynamic-slice_fusion.15
  242.8 3.9 reshape.503
  246.7 5.3 fusion.85
  253.8 12.1 %fusion.86 = (f32[4,6,8,16]{3,2,1,0:T(8,128)S(1)}, f32[4,6,8,16,14,16]{3,5,4,2,1,0:T(8,128)}) fusion(f32[4,14,16]{2,1,0:T(8,128)S(1)} %copy.235, f32[8,16,14,16]{1,3,2,0:T(8,128)S(1)} %get-tuple-element.250, bf16[14,4,16,6,64]{4,3,2,1,0:T(8,128)(2,1)} %get-tuple-element.252, bf16[4,8,4,16,6,64]{5,3,2,1,0,4:T(8,128)(2,1)} %get-tuple-element.296, ...), kind=kOutput, calls=%fused_computation.6.clone.1 | convolution fusion | flops 90141696 | bytes 5504516 | tf_op jit(solution)/shard_map/while/body/eval_jaxpr/rbchd,sbkhd->bhrcsk/dot_general | solution.py:150
  268.2 5.2 fusion.87
  273.4 12.7 %fusion.88 = f32[4,6,64,8,16,1]{2,4,5,3,1,0:T(8,128)} fusion(f32[4,6,8,16,14,16]{3,5,4,2,1,0:T(8,128)} %get-tuple-element.253, f32[4,14,16]{2,1,0:T(8,128)S(1)} %copy.235, f32[8,16,14,16]{1,3,2,0:T(8,128)S(1)} %get-tuple-element.250, bf16[14,4,16,6,64]{4,3,2,1,0:T(8,128)(2,1)} %get-tuple-element.255), kind=kOutput, calls=%fused_computation.8.clone.1 | convolution fusion | flops 90144768 | bytes 4345344 | tf_op jit(solution)/shard_map/while/body/eval_jaxpr/bhrcsk,sbkhd->rbchd/dot_general | solution.py:155
  286.1 12.2 %fusion.89 = (f32[4,6,8,16]{3,2,1,0:T(8,128)S(1)}, f32[4,6,8,16,14,16]{3,5,4,2,1,0:T(8,128)}) fusion(f32[4,14,16]{2,1,0:T(8,128)S(1)} %copy.236, f32[8,16,14,16]{1,3,2,0:T(8,128)S(1)} %get-tuple-element.257, bf16[14,4,16,6,64]{4,3,2,1,0:T(8,128)(2,1)} %get-tuple-element.258, bf16[4,8,4,16,6,64]{5,3,2,1,0,4:T(8,128)(2,1)} %get-tuple-element.296, ...), kind=kOutput, calls=%fused_computation.4.clone.1 | convolution fusion | flops 90141696 | bytes 5504516 | tf_op jit(solution)/shard_map/while/body/eval_jaxpr/rbchd,sbkhd->bhrcsk/dot_general | solution.py:150
  298.3 12.8 %fusion.90 = f32[8,4,16,6,64]{4,2,0,3,1:T(8,128)} fusion(f32[4,6,64,8,16,1]{2,4,5,3,1,0:T(8,128)S(1)} %copy-done.4, f32[4,6,8,16,14,16]{3,5,4,2,1,0:T(8,128)} %get-tuple-element.259, f32[4,14,16]{2,1,0:T(8,128)S(1)} %copy.236, f32[8,16,14,16]{1,3,2,0:T(8,128)S(1)} %get-tuple-element.257, bf16[14,4,16,6,64]{4,3,2,1,0:T(8,128)(2,1)} %get-tuple-element.260), kind=kOutput, calls=%fused_computation.11.clone.1 | convolution fusion | flops 90341376 | bytes 5131776 | tf_op jit(solution)/shard_map/while/body/eval_jaxpr/bhrcsk,sbkhd->rbchd/dot_general | solution.py:155
  319.7 3.9 reshape.503
  323.7 5.3 fusion.85
  330.8 12.1 %fusion.86 = (f32[4,6,8,16]{3,2,1,0:T(8,128)S(1)}, f32[4,6,8,16,14,16]{3,5,4,2,1,0:T(8,128)}) fusion(f32[4,14,16]{2,1,0:T(8,128)S(1)} %copy.235, f32[8,16,14,16]{1,3,2,0:T(8,128)S(1)} %get-tuple-element.250, bf16[14,4,16,6,64]{4,3,2,1,0:T(8,128)(2,1)} %get-tuple-element.252, bf16[4,8,4,16,6,64]{5,3,2,1,0,4:T(8,128)(2,1)} %get-tuple-element.296, ...), kind=kOutput, calls=%fused_computation.6.clone.1 | convolution fusion | flops 90141696 | bytes 5504516 | tf_op jit(solution)/shard_map/while/body/eval_jaxpr/rbchd,sbkhd->bhrcsk/dot_general | solution.py:150
  345.1 5.2 fusion.87
  350.4 12.7 %fusion.88 = f32[4,6,64,8,16,1]{2,4,5,3,1,0:T(8,128)} fusion(f32[4,6,8,16,14,16]{3,5,4,2,1,0:T(8,128)} %get-tuple-element.253, f32[4,14,16]{2,1,0:T(8,128)S(1)} %copy.235, f32[8,16,14,16]{1,3,2,0:T(8,128)S(1)} %get-tuple-element.250, bf16[14,4,16,6,64]{4,3,2,1,0:T(8,128)(2,1)} %get-tuple-element.255), kind=kOutput, calls=%fused_computation.8.clone.1 | convolution fusion | flops 90144768 | bytes 4345344 | tf_op jit(solution)/shard_map/while/body/eval_jaxpr/bhrcsk,sbkhd->rbchd/dot_general | solution.py:155
  363.1 12.2 %fusion.89 = (f32[4,6,8,16]{3,2,1,0:T(8,128)S(1)}, f32[4,6,8,16,14,16]{3,5,4,2,1,0:T(8,128)}) fusion(f32[4,14,16]{2,1,0:T(8,128)S(1)} %copy.236, f32[8,16,14,16]{1,3,2,0:T(8,128)S(1)} %get-tuple-element.257, bf16[14,4,16,6,64]{4,3,2,1,0:T(8,128)(2,1)} %get-tuple-element.258, bf16[4,8,4,16,6,64]{5,3,2,1,0,4:T(8,128)(2,1)} %get-tuple-element.296, ...), kind=kOutput, calls=%fused_computation.4.clone.1 | convolution fusion | flops 90141696 | bytes 5504516 | tf_op jit(solution)/shard_map/while/body/eval_jaxpr/rbchd,sbkhd->bhrcsk/dot_general | solution.py:150
  375.3 12.8 %fusion.90 = f32[8,4,16,6,64]{4,2,0,3,1:T(8,128)} fusion(f32[4,6,64,8,16,1]{2,4,5,3,1,0:T(8,128)S(1)} %copy-done.4, f32[4,6,8,16,14,16]{3,5,4,2,1,0:T(8,128)} %get-tuple-element.259, f32[4,14,16]{2,1,0:T(8,128)S(1)} %copy.236, f32[8,16,14,16]{1,3,2,0:T(8,128)S(1)} %get-tuple-element.257, bf16[14,4,16,6,64]{4,3,2,1,0:T(8,128)(2,1)} %get-tuple-element.260), kind=kOutput, calls=%fused_computation.11.clone.1 | convolution fusion | flops 90341376 | bytes 5131776 | tf_op jit(solution)/shard_map/while/body/eval_jaxpr/bhrcsk,sbkhd->rbchd/dot_general | solution.py:155
  396.7 3.9 reshape.503
  400.7 5.3 fusion.85
  407.8 12.1 %fusion.86 = (f32[4,6,8,16]{3,2,1,0:T(8,128)S(1)}, f32[4,6,8,16,14,16]{3,5,4,2,1,0:T(8,128)}) fusion(f32[4,14,16]{2,1,0:T(8,128)S(1)} %copy.235, f32[8,16,14,16]{1,3,2,0:T(8,128)S(1)} %get-tuple-element.250, bf16[14,4,16,6,64]{4,3,2,1,0:T(8,128)(2,1)} %get-tuple-element.252, bf16[4,8,4,16,6,64]{5,3,2,1,0,4:T(8,128)(2,1)} %get-tuple-element.296, ...), kind=kOutput, calls=%fused_computation.6.clone.1 | convolution fusion | flops 90141696 | bytes 5504516 | tf_op jit(solution)/shard_map/while/body/eval_jaxpr/rbchd,sbkhd->bhrcsk/dot_general | solution.py:150
  422.1 5.2 fusion.87
  427.4 12.7 %fusion.88 = f32[4,6,64,8,16,1]{2,4,5,3,1,0:T(8,128)} fusion(f32[4,6,8,16,14,16]{3,5,4,2,1,0:T(8,128)} %get-tuple-element.253, f32[4,14,16]{2,1,0:T(8,128)S(1)} %copy.235, f32[8,16,14,16]{1,3,2,0:T(8,128)S(1)} %get-tuple-element.250, bf16[14,4,16,6,64]{4,3,2,1,0:T(8,128)(2,1)} %get-tuple-element.255), kind=kOutput, calls=%fused_computation.8.clone.1 | convolution fusion | flops 90144768 | bytes 4345344 | tf_op jit(solution)/shard_map/while/body/eval_jaxpr/bhrcsk,sbkhd->rbchd/dot_general | solution.py:155
  440.1 12.2 %fusion.89 = (f32[4,6,8,16]{3,2,1,0:T(8,128)S(1)}, f32[4,6,8,16,14,16]{3,5,4,2,1,0:T(8,128)}) fusion(f32[4,14,16]{2,1,0:T(8,128)S(1)} %copy.236, f32[8,16,14,16]{1,3,2,0:T(8,128)S(1)} %get-tuple-element.257, bf16[14,4,16,6,64]{4,3,2,1,0:T(8,128)(2,1)} %get-tuple-element.258, bf16[4,8,4,16,6,64]{5,3,2,1,0,4:T(8,128)(2,1)} %get-tuple-element.296, ...), kind=kOutput, calls=%fused_computation.4.clone.1 | convolution fusion | flops 90141696 | bytes 5504516 | tf_op jit(solution)/shard_map/while/body/eval_jaxpr/rbchd,sbkhd->bhrcsk/dot_general | solution.py:150
  452.3 12.8 %fusion.90 = f32[8,4,16,6,64]{4,2,0,3,1:T(8,128)} fusion(f32[4,6,64,8,16,1]{2,4,5,3,1,0:T(8,128)S(1)} %copy-done.4, f32[4,6,8,16,14,16]{3,5,4,2,1,0:T(8,128)} %get-tuple-element.259, f32[4,14,16]{2,1,0:T(8,128)S(1)} %copy.236, f32[8,16,14,16]{1,3,2,0:T(8,128)S(1)} %get-tuple-element.257, bf16[14,4,16,6,64]{4,3,2,1,0:T(8,128)(2,1)} %get-tuple-element.260), kind=kOutput, calls=%fused_computation.11.clone.1 | convolution fusion | flops 90341376 | bytes 5131776 | tf_op jit(solution)/shard_map/while/body/eval_jaxpr/bhrcsk,sbkhd->rbchd/dot_general | solution.py:155
  473.7 3.9 reshape.503
  477.6 5.3 fusion.85
  484.8 12.1 %fusion.86 = (f32[4,6,8,16]{3,2,1,0:T(8,128)S(1)}, f32[4,6,8,16,14,16]{3,5,4,2,1,0:T(8,128)}) fusion(f32[4,14,16]{2,1,0:T(8,128)S(1)} %copy.235, f32[8,16,14,16]{1,3,2,0:T(8,128)S(1)} %get-tuple-element.250, bf16[14,4,16,6,64]{4,3,2,1,0:T(8,128)(2,1)} %get-tuple-element.252, bf16[4,8,4,16,6,64]{5,3,2,1,0,4:T(8,128)(2,1)} %get-tuple-element.296, ...), kind=kOutput, calls=%fused_computation.6.clone.1 | convolution fusion | flops 90141696 | bytes 5504516 | tf_op jit(solution)/shard_map/while/body/eval_jaxpr/rbchd,sbkhd->bhrcsk/dot_general | solution.py:150
  499.1 5.2 fusion.87
  504.4 12.7 %fusion.88 = f32[4,6,64,8,16,1]{2,4,5,3,1,0:T(8,128)} fusion(f32[4,6,8,16,14,16]{3,5,4,2,1,0:T(8,128)} %get-tuple-element.253, f32[4,14,16]{2,1,0:T(8,128)S(1)} %copy.235, f32[8,16,14,16]{1,3,2,0:T(8,128)S(1)} %get-tuple-element.250, bf16[14,4,16,6,64]{4,3,2,1,0:T(8,128)(2,1)} %get-tuple-element.255), kind=kOutput, calls=%fused_computation.8.clone.1 | convolution fusion | flops 90144768 | bytes 4345344 | tf_op jit(solution)/shard_map/while/body/eval_jaxpr/bhrcsk,sbkhd->rbchd/dot_general | solution.py:155
  517.1 12.2 %fusion.89 = (f32[4,6,8,16]{3,2,1,0:T(8,128)S(1)}, f32[4,6,8,16,14,16]{3,5,4,2,1,0:T(8,128)}) fusion(f32[4,14,16]{2,1,0:T(8,128)S(1)} %copy.236, f32[8,16,14,16]{1,3,2,0:T(8,128)S(1)} %get-tuple-element.257, bf16[14,4,16,6,64]{4,3,2,1,0:T(8,128)(2,1)} %get-tuple-element.258, bf16[4,8,4,16,6,64]{5,3,2,1,0,4:T(8,128)(2,1)} %get-tuple-element.296, ...), kind=kOutput, calls=%fused_computation.4.clone.1 | convolution fusion | flops 90141696 | bytes 5504516 | tf_op jit(solution)/shard_map/while/body/eval_jaxpr/rbchd,sbkhd->bhrcsk/dot_general | solution.py:150
  529.3 12.8 %fusion.90 = f32[8,4,16,6,64]{4,2,0,3,1:T(8,128)} fusion(f32[4,6,64,8,16,1]{2,4,5,3,1,0:T(8,128)S(1)} %copy-done.4, f32[4,6,8,16,14,16]{3,5,4,2,1,0:T(8,128)} %get-tuple-element.259, f32[4,14,16]{2,1,0:T(8,128)S(1)} %copy.236, f32[8,16,14,16]{1,3,2,0:T(8,128)S(1)} %get-tuple-element.257, bf16[14,4,16,6,64]{4,3,2,1,0:T(8,128)(2,1)} %get-tuple-element.260), kind=kOutput, calls=%fused_computation.11.clone.1 | convolution fusion | flops 90341376 | bytes 5131776 | tf_op jit(solution)/shard_map/while/body/eval_jaxpr/bhrcsk,sbkhd->rbchd/dot_general | solution.py:155
  545.4 16.1 %exponential_reduce_fusion = (f32[32,6,128]{2,1,0:T(8,128)S(1)}, f32[32,6,128,128]{2,3,1,0:T(8,128)}) fusion(bf16[32,128,6,64]{1,3,2,0:T(8,128)(2,1)} %bitcast.19, bf16[32,128,6,64]{3,2,0,1:T(8,128)(2,1)} %reshape.498), kind=kOutput, calls=%fused_computation.28 | convolution fusion | flops 405774336 | bytes 18972672 | tf_op jit(solution)/shard_map/sqhd,skhd->shqk/dot_general | solution.py:213
  561.6 9.9 %fusion.19 = f32[32,128,6,64]{1,3,2,0:T(8,128)} fusion(bf16[32,128,6,64]{1,3,2,0:T(8,128)(2,1)} %bitcast.11, f32[32,6,128,128]{2,3,1,0:T(8,128)} %get-tuple-element.175), kind=kOutput, calls=%fused_computation.46 | convolution fusion | flops 405798912 | bytes 22020096 | tf_op jit(solution)/shard_map/shqk,skhd->sqhd/dot_general | solution.py:218
  571.5 12.7 %copy.186 = f32[32,128,6,64]{3,0,2,1:T(8,128)} copy(f32[32,128,6,64]{1,3,2,0:T(8,128)} %fusion.19) | data formatting | bytes 12582912 | tf_op jit(solution)/shard_map/reshape | solution.py:228
  584.2 9.3 %convolution_bitcast_fusion = f32[4,8,4,16,6,64]{5,2,0,4,3,1:T(4,128)S(1)} fusion(f32[32,8,16,6,64,1]{4,0,5,3,2,1:T(8,128)} %bitcast.170, pred[4,4,32,1,1,1]{2,1,0,5,4,3:T(4,128)(4,1)S(1)} %bitcast.180), kind=kOutput, calls=%fused_computation.47 | convolution fusion | flops 301989888 | bytes 9437696 | tf_op jit(solution)/shard_map/abs,srchd->arbchd/dot_general | solution.py:225
  593.5 6.3 %copy.163 = f32[4,8,4,16,6,64]{5,3,2,4,1,0:T(8,128)} copy(f32[4,8,4,16,6,64]{5,2,0,4,3,1:T(4,128)S(1)} %convolution_bitcast_fusion) | data formatting | bytes 6291456 | tf_op jit(solution)/shard_map/abs,srchd->arbchd/transpose | solution.py:225
  602.0 7.7 %fusion.15 = bf16[4,8,64,6,64]{4,2,3,1,0:T(8,128)(2,1)} fusion(f32[4,8,64,6,64]{4,2,3,1,0:T(8,128)} %get-tuple-element.56, f32[4,8,4,16,6,64]{5,3,2,4,1,0:T(8,128)} %copy.163, f32[4,8,64,6]{2,3,1,0:T(8,128)S(1)} %copy.166), kind=kLoop, calls=%fused_computation.33 | loop fusion | flops 2359296 | bytes 7913472 | tf_op jit(solution)/shard_map/convert_element_type | solution.py:241
  609.7 4.2 copy.167
  614.0 3.4 reshape.463
  617.4 4.3 fusion.18
  (166 shorter events, 70.2 us)
Async XLA Ops:
  0.0 169.9 %copy-start = (bf16[384,384]{1,0:T(8,128)(2,1)S(1)}, bf16[384,384]{1,0:T(8,128)(2,1)}, u32[]{:S(2)}) copy-start(bf16[384,384]{1,0:T(8,128)(2,1)} %param.15) | copy-start | bytes 884740
  0.0 8.3 %copy-start.10 = (s32[4,4]{1,0:T(4,128)S(1)}, s32[4,4]{1,0:T(4,128)}, u32[]{:S(2)}) copy-start(s32[4,4]{1,0:T(4,128)} %param.18) | copy-start | bytes 196
  0.0 14.8 %copy-start.7 = (s32[4,4,4]{2,1,0:T(4,128)S(1)}, s32[4,4,4]{2,1,0:T(4,128)}, u32[]{:S(2)}) copy-start(s32[4,4,4]{2,1,0:T(4,128)} %param.19) | copy-start | bytes 772
  0.0 20.4 %copy-start.5 = (bf16[384,384]{1,0:T(8,128)(2,1)S(1)}, bf16[384,384]{1,0:T(8,128)(2,1)}, u32[]{:S(2)}) copy-start(bf16[384,384]{1,0:T(8,128)(2,1)} %param.13) | copy-start | bytes 884740
  3.8 19.6 %copy-start.6 = (bf16[384,384]{1,0:T(8,128)(2,1)S(1)}, bf16[384,384]{1,0:T(8,128)(2,1)}, u32[]{:S(2)}) copy-start(bf16[384,384]{1,0:T(8,128)(2,1)} %param.14) | copy-start | bytes 884740
  3.8 20.5 %collective-permute-start.1 = (bf16[32,3,384]{2,1,0:T(4,128)(2,1)S(1)}, bf16[32,3,384]{2,1,0:T(4,128)(2,1)S(1)}, u32[]{:S(2)}, u32[]{:S(2)}) collective-permute-start(bf16[32,3,384]{2,1,0:T(4,128)(2,1)S(1)} %get-tuple-element.163), channel_id=1, source_target_pairs={{4,0},{8,4},{12,8},{5,1},{9,5},{13,9},{6,2},{10,6},{14,10},{7,3},{... | collective-permute-start | bytes 221192 | tf_op jit(solution)/shard_map/ppermute | solution.py:22
  5.3 19.0 %collective-permute-start = (bf16[32,3,384]{2,1,0:T(4,128)(2,1)S(1)}, bf16[32,3,384]{2,1,0:T(4,128)(2,1)S(1)}, u32[]{:S(2)}, u32[]{:S(2)}) collective-permute-start(bf16[32,3,384]{2,1,0:T(4,128)(2,1)S(1)} %get-tuple-element.162), channel_id=1, source_target_pairs={{0,4},{4,8},{8,12},{1,5},{5,9},{9,13},{2,6},{6,10},{10,14},{3,7},{... | collective-permute-start | bytes 221192 | tf_op jit(solution)/shard_map/ppermute | solution.py:19
  9.2 117.9 %collective-permute-start.5 = (bf16[32,3]{1,0:T(8,128)(2,1)}, bf16[32,3]{1,0:T(8,128)(2,1)}, u32[]{:S(2)}, u32[]{:S(2)}) collective-permute-start(bf16[32,3]{1,0:T(8,128)(2,1)} %get-tuple-element.167), channel_id=1, source_target_pairs={{4,0},{8,4},{12,8},{5,1},{9,5},{13,9},{6,2},{10,6},{14,10},{7,3},{... | collective-permute-start | bytes 584 | tf_op jit(solution)/shard_map/ppermute | solution.py:22
  10.5 116.6 %collective-permute-start.4 = (bf16[32,3]{1,0:T(8,128)(2,1)}, bf16[32,3]{1,0:T(8,128)(2,1)}, u32[]{:S(2)}, u32[]{:S(2)}) collective-permute-start(bf16[32,3]{1,0:T(8,128)(2,1)} %get-tuple-element.166), channel_id=1, source_target_pairs={{0,4},{4,8},{8,12},{1,5},{5,9},{9,13},{2,6},{6,10},{10,14},{3,7},{... | collective-permute-start | bytes 584 | tf_op jit(solution)/shard_map/ppermute | solution.py:19
  14.8 0.5 copy-start.13
  15.3 0.5 copy-start.11
  17.2 6.9 %all-to-all-start = ((s32[4,1,8]{2,1,0:T(1,128)}), s32[4,1,8]{2,1,0:T(1,128)S(1)}, u32[]{:S(2)}, u32[]{:S(2)}) async-start(s32[4,1,8]{2,1,0:T(1,128)} %bitcast.8), calls=%async_computation | async-start | bytes 4096 | tf_op jit(solution)/shard_map/all_to_all | solution.py:185
  24.4 8.8 %collective-permute-start.3 = (bf16[3,70,384]{2,1,0:T(8,128)(2,1)S(1)}, bf16[3,70,384]{2,1,0:T(8,128)(2,1)S(1)}, u32[]{:S(2)}, u32[]{:S(2)}) collective-permute-start(bf16[3,70,384]{2,1,0:T(8,128)(2,1)S(1)} %get-tuple-element.161), channel_id=1, source_target_pairs={{1,0},{2,1},{3,2},{5,4},{6,5},{7,6},{9,8},{10,9},{11,10},{13,12},{... | collective-permute-start | bytes 483848 | tf_op jit(solution)/shard_map/ppermute | solution.py:22
  26.8 8.5 %collective-permute-start.2 = (bf16[3,70,384]{2,1,0:T(8,128)(2,1)S(1)}, bf16[3,70,384]{2,1,0:T(8,128)(2,1)S(1)}, u32[]{:S(2)}, u32[]{:S(2)}) collective-permute-start(bf16[3,70,384]{2,1,0:T(8,128)(2,1)S(1)} %get-tuple-element.160), channel_id=1, source_target_pairs={{0,1},{1,2},{2,3},{4,5},{5,6},{6,7},{8,9},{9,10},{10,11},{12,13},{... | collective-permute-start | bytes 483848 | tf_op jit(solution)/shard_map/ppermute | solution.py:19
  102.1 4.8 copy-start.15
  102.1 130.4 %all-to-all-start.2 = ((bf16[4,8,128,384]{2,3,1,0:T(8,128)(2,1)}), bf16[4,8,128,384]{2,3,1,0:T(8,128)(2,1)}, u32[]{:S(2)}, u32[]{:S(2)}) async-start(bf16[4,8,128,384]{2,3,1,0:T(8,128)(2,1)} %copy.158), calls=%async_computation.2 | async-start | bytes 6291456 | tf_op jit(solution)/shard_map/all_to_all | solution.py:186
  116.3 6.1 copy-start.14
  116.3 6.1 copy-start.12
  122.5 4.5 copy-start.8
  127.8 37.3 %collective-permute-start.7 = (bf16[3,70]{1,0:T(4,128)(2,1)S(1)}, bf16[3,70]{1,0:T(4,128)(2,1)S(1)}, u32[]{:S(2)}, u32[]{:S(2)}) collective-permute-start(bf16[3,70]{1,0:T(4,128)(2,1)S(1)} %get-tuple-element.165), channel_id=1, source_target_pairs={{1,0},{2,1},{3,2},{5,4},{6,5},{7,6},{9,8},{10,9},{11,10},{13,12},{... | collective-permute-start | bytes 1268 | tf_op jit(solution)/shard_map/ppermute | solution.py:22
  129.8 35.4 %collective-permute-start.6 = (bf16[3,70]{1,0:T(4,128)(2,1)S(1)}, bf16[3,70]{1,0:T(4,128)(2,1)S(1)}, u32[]{:S(2)}, u32[]{:S(2)}) collective-permute-start(bf16[3,70]{1,0:T(4,128)(2,1)S(1)} %get-tuple-element.164), channel_id=1, source_target_pairs={{0,1},{1,2},{2,3},{4,5},{5,6},{6,7},{8,9},{9,10},{10,11},{12,13},{... | collective-permute-start | bytes 1268 | tf_op jit(solution)/shard_map/ppermute | solution.py:19
  178.3 2.4 copy-start.2
  180.7 2.4 copy-start.3
  232.5 329.0 %all-to-all-start.1 = ((bf16[4,8,128,384]{2,3,1,0:T(8,128)(2,1)}), bf16[4,8,128,384]{2,3,1,0:T(8,128)(2,1)}, u32[]{:S(2)}, u32[]{:S(2)}) async-start(bf16[4,8,128,384]{2,3,1,0:T(8,128)(2,1)} %copy.151), calls=%async_computation.1 | async-start | bytes 6291456 | tf_op jit(solution)/shard_map/all_to_all | solution.py:193
  286.1 12.2 %copy-start.4 = (f32[4,6,64,8,16,1]{2,4,5,3,1,0:T(8,128)S(1)}, f32[4,6,64,8,16,1]{2,4,5,3,1,0:T(8,128)}, u32[]{:S(2)}) copy-start(f32[4,6,64,8,16,1]{2,4,5,3,1,0:T(8,128)} %fusion.88) | copy-start | bytes 2359300 | tf_op jit(solution)/shard_map/while
  363.1 12.2 %copy-start.4 = (f32[4,6,64,8,16,1]{2,4,5,3,1,0:T(8,128)S(1)}, f32[4,6,64,8,16,1]{2,4,5,3,1,0:T(8,128)}, u32[]{:S(2)}) copy-start(f32[4,6,64,8,16,1]{2,4,5,3,1,0:T(8,128)} %fusion.88) | copy-start | bytes 2359300 | tf_op jit(solution)/shard_map/while
  440.1 12.2 %copy-start.4 = (f32[4,6,64,8,16,1]{2,4,5,3,1,0:T(8,128)S(1)}, f32[4,6,64,8,16,1]{2,4,5,3,1,0:T(8,128)}, u32[]{:S(2)}) copy-start(f32[4,6,64,8,16,1]{2,4,5,3,1,0:T(8,128)} %fusion.88) | copy-start | bytes 2359300 | tf_op jit(solution)/shard_map/while
  517.1 12.2 %copy-start.4 = (f32[4,6,64,8,16,1]{2,4,5,3,1,0:T(8,128)S(1)}, f32[4,6,64,8,16,1]{2,4,5,3,1,0:T(8,128)}, u32[]{:S(2)}) copy-start(f32[4,6,64,8,16,1]{2,4,5,3,1,0:T(8,128)} %fusion.88) | copy-start | bytes 2359300 | tf_op jit(solution)/shard_map/while
  571.5 12.7 %copy-start.9 = (pred[16,32]{1,0:T(8,128)(4,1)S(1)}, pred[16,32]{1,0:T(8,128)(4,1)}, u32[]{:S(2)}) copy-start(pred[16,32]{1,0:T(8,128)(4,1)} %copy-done.8) | copy-start | bytes 1540
  614.0 7.7 %copy-start.1 = (bf16[384,384]{1,0:T(8,128)(2,1)S(1)}, bf16[384,384]{1,0:T(8,128)(2,1)}, u32[]{:S(2)}) copy-start(bf16[384,384]{1,0:T(8,128)(2,1)} %param.15) | copy-start | bytes 884740
where the time goes:
time: 634 us; the launch traced here: 622 us
  local copies, waits for them, and re-layouts  281 us (44%)
  matrix products  254 us (40%)
  starting transfers between devices  49.6 us (8%)
  other arithmetic  21.7 us (3%)
  loops' own time  10.6 us (2%)
    dot_general x8, matrix products, near_row(): jnp.einsum('bhrcsk,sbkhd->rbchd', weights.astype(jnp.bfloat16), value_par...  102 us
    dot_general x8, matrix products, near_row(): jnp.einsum('rbchd,sbkhd->bhrcsk', query_strip, key_part, preferred_elemen...  97.1 us
    gather x2, local copies, waits for them, and re-layouts, pick_tiles(): picked = source_grid[row_pick, col_pick]  89.4 us
    ppermute x4, starting transfers between devices, extended(): lax.ppermute(lax.slice_in_dim(block, block.shape[dim] - width, None, axis...  30 us
    slice x4, local copies, waits for them, and re-layouts, near_row(): key_part = key_strip[:, half:half + tile_cols]  21.1 us
    slice x4, local copies, waits for them, and re-layouts, near_row(): value_part = value_strip[:, half:half + tile_cols]  21 us
    convert_element_type x4, local copies, waits for them, and re-layouts, unit_heads(): return (split_heads * inverse_len * head_factor[:, None]).reshape(project...  20.6 us
    dot_general x1, matrix products, body(): jnp.einsum('sqhd,skhd->shqk', slot_queries, far_keys, preferred_element_t...  16.1 us
  transfers between devices with their start and end apart: 11, of which 3 were waited for; matrix products, arithmetic and copies ran while one was open for 79% of the time, Pallas kernels for 0%

commit v1 on v0

v1 whole, which is shorter than its diff:
```python
import functools
import math
import jax
import jax.numpy as jnp
from jax import lax
from jax.experimental import pallas as pl
from jax.experimental.pallas import tpu as pltpu
from jax.sharding import PartitionSpec as P

HEADS = 6
TILE_ROWS = 8
TILE_COLS = 16
RADIUS = 3
S_MAX = 4
MASK_MOST = 8
SIDE = 8
MARK = 1024.0
MARK_LEVEL = 1000.0
LATE_TILES = 4
LOG2E = math.log2(math.e)
F32 = jnp.float32
BF16 = jnp.bfloat16


def pair_swap(low, high, axis):
    count = lax.axis_size(axis)
    index = lax.axis_index(axis)
    even = index % 2 == 0
    first = [(i, i + 1) for i in range(0, count - 1, 2)]
    second = [(i, i + 1) for i in range(1, count - 1, 2)]
    both = lambda pairs: pairs + [(b, a) for a, b in pairs]
    one = lax.ppermute(jnp.where(even, high, low), axis, both(first))
    two = lax.ppermute(jnp.where(even, low, high), axis, both(second))
    mark = jnp.asarray(MARK, low.dtype)
    before = jnp.where(index == 0, mark, jnp.where(even, two, one))
    after = jnp.where(index == count - 1, mark, jnp.where(even, one, two))
    return before, after


def spread(array, axis):
    count = lax.axis_size(axis)
    held = {0: array}
    bit = count // 2
    while bit:
        pairs = [(i, i ^ bit) for i in range(count)]
        held.update({rel ^ bit: lax.ppermute(item, axis, pairs) for rel, item in held.items()})
        bit //= 2
    return held


def pack_kernel(tile_cols, keep, counts_ref, tokens_ref, *chunk_refs):
    tile_rows = tokens_ref.shape[0] // TILE_ROWS
    free = jnp.int32(0)
    for t in range(tile_rows * tile_cols):
        free = free + (counts_ref[t // tile_cols, t % tile_cols] == 0).astype(jnp.int32)
    seen_free = jnp.int32(0)
    seen_masked = jnp.int32(0)
    for t in range(tile_rows * tile_cols):
        a, b = t // tile_cols, t % tile_cols
        is_free = (counts_ref[a, b] == 0).astype(jnp.int32)
        rank = jnp.where(is_free == 1, seen_free, free + seen_masked)
        seen_free = seen_free + is_free
        seen_masked = seen_masked + 1 - is_free
        low = 0
        for ref in chunk_refs:
            size = ref.shape[0]

            @pl.when((rank >= low) & (rank < low + size))
            def _(ref=ref, low=low, a=a, b=b, rank=rank):
                ref[rank - low] = tokens_ref[
                    TILE_ROWS * a : TILE_ROWS * (a + 1), TILE_COLS * b : TILE_COLS * (b + 1), :
                ].reshape(TILE_ROWS * TILE_COLS, tokens_ref.shape[-1])

            low += size


def head_blocks(feature):
    size = feature // HEADS
    row = lax.broadcasted_iota(jnp.int32, (feature, feature), 0) // size
    col = lax.broadcasted_iota(jnp.int32, (feature, feature), 1) // size
    return jnp.where(row == col, 1.0, 0.0).astype(BF16)


def unit(projected, blocks):
    squares = (projected * projected).astype(BF16)
    total = jnp.dot(squares, blocks, preferred_element_type=F32)
    return projected * lax.rsqrt(total + 1e-6)


def normed_of(raw, gain):
    level = jnp.mean(raw * raw, axis=-1, keepdims=True)
    return raw * lax.rsqrt(level + 1e-6) * gain, level


def contract_last(left, right):
    return lax.dot_general(left, right, (((1,), (1,)), ((), ())), preferred_element_type=F32)


def near_kernel(
    counts_ref, tokens_ref, tail_ref, top_ref, bottom_ref, gain_ref, scale_ref,
    wq_ref, wk_ref, wv_ref, wo_ref,
    out_ref, acc_ref, mq_ref,
    keys, values, valid, queries, blocks,
):
    grid_rows, grid_cols, feature = tokens_ref.shape
    tile_rows = grid_rows // TILE_ROWS
    tile_cols = grid_cols // TILE_COLS
    wide = tail_ref.shape[1] + grid_cols
    lanes = 2 * feature // HEADS
    win_rows = TILE_ROWS + 2 * RADIUS
    blocks[...] = head_blocks(feature)

    def put_keys(raw, own_valid, places):
        rows = raw.shape[0]
        normed, level = normed_of(raw, gain_ref[...][None])
        ok = jnp.where(level < MARK_LEVEL, own_valid, 0.0)
        ok = pltpu.roll(jnp.broadcast_to(ok, (rows, wide, lanes)), RADIUS, 1)
        shifted = pltpu.roll(normed, RADIUS, 1).astype(BF16).reshape(rows * wide, feature)
        key = unit(jnp.dot(shifted, wk_ref[...], preferred_element_type=F32), blocks[...])
        value = jnp.dot(shifted, wv_ref[...], preferred_element_type=F32)
        value = value * jnp.concatenate([ok] * (feature // lanes), axis=-1).reshape(value.shape)
        key = key.reshape(rows, wide, feature)
        value = value.reshape(rows, wide, feature)
        for side in range(2):
            low = side * SIDE
            for at, start, size in places:
                into = (side, pl.ds(at, size))
                keys[into] = key[start : start + size, low : low + grid_cols].astype(BF16)
                values[into] = value[start : start + size, low : low + grid_cols].astype(BF16)
                valid[into] = ok[start : start + size, low : low + grid_cols].astype(BF16)
        return normed

    edge = jnp.concatenate([top_ref[...], bottom_ref[...]], axis=0).astype(F32)
    put_keys(edge, 1.0, ((0, 0, RADIUS), (RADIUS + grid_rows, RADIUS, RADIUS)))

    def project(a, carry):
        rows = pl.ds(a * TILE_ROWS, TILE_ROWS)
        raw = jnp.concatenate([tokens_ref[rows], tail_ref[rows]], axis=1).astype(F32)
        tile = lax.broadcasted_iota(jnp.int32, (1, wide, 1), 1) // TILE_COLS
        own_valid = jnp.ones((1, wide, 1), F32)
        for b in range(tile_cols):
            flag = jnp.where(counts_ref[a, b] == 0, 1.0, 0.0)
            own_valid = jnp.where(tile == b, flag, own_valid)
        normed = put_keys(raw, own_valid, ((RADIUS + a * TILE_ROWS, 0, TILE_ROWS),))
        flat = normed[:, :grid_cols].astype(BF16).reshape(TILE_ROWS * grid_cols, feature)
        query = unit(jnp.dot(flat, wq_ref[...], preferred_element_type=F32), blocks[...])
        query = (query * scale_ref[...]).reshape(TILE_ROWS, grid_cols // SIDE, SIDE, feature)
        for c in range(grid_cols // SIDE):
            queries[a, c] = query[:, c].reshape(TILE_ROWS * SIDE, feature).astype(BF16)
        return carry

    lax.fori_loop(0, tile_rows, project, 0)

    tokens_of_side = TILE_ROWS * SIDE
    window = win_rows * TILE_COLS
    qpos = lax.broadcasted_iota(jnp.int32, (2 * tokens_of_side, window), 0) % tokens_of_side
    kpos = lax.broadcasted_iota(jnp.int32, (2 * tokens_of_side, window), 1)
    down = kpos // TILE_COLS - qpos // SIDE
    across = kpos % TILE_COLS - qpos % SIDE
    inside = (down >= 0) & (down <= 2 * RADIUS) & (across >= 0) & (across <= 2 * RADIUS)
    band = jnp.where(inside, 1.0, 0.0).astype(BF16)
    first = lax.broadcasted_iota(jnp.int32, (tokens_of_side, lanes), 1) < lanes // 2
    zero = jnp.zeros((tokens_of_side, lanes), BF16)

    def attend(t, slot):
        a = t // tile_cols
        b = t % tile_cols
        nums, dens = [], []
        for side in range(2):
            query = queries[a, 2 * b + side]
            at = (side, pl.ds(a * TILE_ROWS, win_rows), pl.ds(pl.multiple_of(b * TILE_COLS, TILE_COLS), TILE_COLS))
            ok = valid[at].reshape(window, lanes)
            num, den = [], []
            for p in range(feature // lanes):
                part = slice(p * lanes, (p + 1) * lanes)
                key = keys[(*at, part)].reshape(window, lanes)
                value = jnp.concatenate([values[(*at, part)].reshape(window, lanes), ok], axis=1)
                q = query[:, part]
                stacked = jnp.concatenate([jnp.where(first, q, zero), jnp.where(first, zero, q)], axis=0)
                weights = jnp.exp2(contract_last(stacked, key)).astype(BF16) * band
                both = jnp.dot(weights, value, preferred_element_type=F32)
                num.append(jnp.where(first, both[:tokens_of_side, :lanes], both[tokens_of_side:, :lanes]))
                den.append(jnp.where(first, both[:tokens_of_side, lanes:], both[tokens_of_side:, lanes:]))
            nums.append(jnp.concatenate(num, axis=1))
            dens.append(jnp.concatenate(den, axis=1))
        masked = counts_ref[a, b] > 0

        @pl.when(masked)
        def _():
            for side in range(2):
                part = slice(side * tokens_of_side, (side + 1) * tokens_of_side)
                acc_ref[slot, 0, part] = nums[side]
                acc_ref[slot, 1, part] = dens[side]
                mq_ref[slot, part] = queries[a, 2 * b + side]

        @pl.when(jnp.logical_not(masked))
        def _():
            finish(a, b, nums, dens, tokens_ref, wo_ref, out_ref.at[
                pl.ds(a * TILE_ROWS, TILE_ROWS), pl.ds(pl.multiple_of(b * TILE_COLS, TILE_COLS), TILE_COLS)])

        return slot + masked.astype(jnp.int32)

    lax.fori_loop(0, tile_rows * tile_cols, attend, jnp.int32(0))


def finish(a, b, nums, dens, tokens_ref, wo_ref, into):
    feature = tokens_ref.shape[-1]
    sides = [(n / d).reshape(TILE_ROWS, SIDE, feature) for n, d in zip(nums, dens)]
    attended = jnp.concatenate(sides, axis=1).reshape(TILE_ROWS * TILE_COLS, feature).astype(BF16)
    raw = tokens_ref[
        pl.ds(a * TILE_ROWS, TILE_ROWS), pl.ds(pl.multiple_of(b * TILE_COLS, TILE_COLS), TILE_COLS)
    ].reshape(TILE_ROWS * TILE_COLS, feature).astype(F32)
    mixed = raw + jnp.dot(attended, wo_ref[...], preferred_element_type=F32)
    into[...] = mixed.astype(BF16).reshape(TILE_ROWS, TILE_COLS, feature)


def far_kernel(plan, last, all_cols, axes, *refs):
    col_count = len(plan["rels"])
    me_ref, counts_ref, sources_ref = refs[:3]
    refs = refs[3:]
    rel_counts = dict(zip(plan["rels"], refs[:col_count]))
    refs = refs[col_count:]
    chunks = list(zip(plan["chunks"], refs[: len(plan["chunks"])]))
    refs = refs[len(plan["chunks"]) :]
    mq_ref, acc_in_ref, gain_ref, wk_ref, wv_ref = refs[:5]
    refs = refs[5:]
    if last:
        tokens_ref, wo_ref, _, out_ref = refs[:4]
        refs = refs[4:]
    else:
        acc_out_ref = refs[0]
        refs = refs[1:]
    keys, values, blocks, raw, acc_ref, needed, place, todo, todo_count, tile_of = refs[:10]
    refs = refs[10:]
    if last:
        staged, sems = refs
    tile_rows, tile_cols = counts_ref.shape
    tiles = tile_rows * tile_cols
    tile_size, feature = raw.shape[1:]
    lanes = 2 * feature // HEADS
    blocks[...] = head_blocks(feature)
    my_col = me_ref[0]
    my_band = me_ref[1]

    def clear(i, carry):
        place[i] = -1
        return carry

    lax.fori_loop(0, col_count * tiles, clear, 0)

    def plan_tile(t, carry):
        count, slot = carry
        a, b = t // tile_cols, t % tile_cols
        live = counts_ref[a, b]

        @pl.when(live > 0)
        def _():
            tile_of[slot] = t
            todo_count[slot] = 0

        def plan_entry(j, count):
            source = sources_ref[a, b, j]
            col = source % all_cols
            rel = (col // tile_cols) ^ my_col
            sa = source // all_cols - my_band * tile_rows
            sb = col % tile_cols
            local = sa * tile_cols + sb

            def rank_in(ref):
                def step(i, rank):
                    return rank + (ref[i // tile_cols, i % tile_cols] == 0).astype(jnp.int32)

                return lax.fori_loop(0, local, step, jnp.int32(0))

            rank = jnp.int32(0)
            for known, ref in rel_counts.items():
                rank = lax.cond(rel == known, functools.partial(rank_in, ref), lambda rank=rank: rank)
            here = jnp.bool_(False)
            for (known, low, size), _ in chunks:
                here = here | ((rel == known) & (rank >= low) & (rank < low + size))
            name = rel * tiles + rank
            fresh = here & (place[name] < 0)

            @pl.when(fresh)
            def _():
                place[name] = count
                needed[count] = name

            @pl.when(here)
            def _():
                n = todo_count[slot]
                todo[slot, n] = place[name]
                todo_count[slot] = n + 1

            return count + fresh.astype(jnp.int32)

        count = lax.fori_loop(0, live, plan_entry, count)
        return count, slot + (live > 0).astype(jnp.int32)

    count, slots = lax.fori_loop(0, tiles, plan_tile, (jnp.int32(0), jnp.int32(0)))

    def fetch(i, k):
        name = needed[i]
        rel, rank = name // tiles, name % tiles
        for (known, low, size), ref in chunks:
            @pl.when((rel == known) & (rank >= low) & (rank < low + size))
            def _(ref=ref, low=low):
                raw[k] = ref[rank - low]

    def project(i, carry):
        fetch(2 * i, 0)
        fetch(jnp.minimum(2 * i + 1, count - 1), 1)
        flat = raw[...].reshape(2 * tile_size, feature).astype(F32)
        normed = normed_of(flat, gain_ref[...])[0].astype(BF16)
        key = unit(jnp.dot(normed, wk_ref[...], preferred_element_type=F32), blocks[...]).astype(BF16)
        value = jnp.dot(normed, wv_ref[...], preferred_element_type=F32).astype(BF16)
        keys[pl.ds(2 * i, 2)] = key.reshape(2, tile_size, feature)
        values[pl.ds(2 * i, 2)] = value.reshape(2, tile_size, feature)
        return carry

    lax.fori_loop(0, (count + 1) // 2, project, 0)

    first = lax.broadcasted_iota(jnp.int32, (tile_size, lanes), 1) < lanes // 2
    zero = jnp.zeros((tile_size, lanes), BF16)

    def attend(slot, carry):
        have = todo_count[slot]
        acc_ref[...] = acc_in_ref[slot]

        def step(i, carry):
            two = 2 * i + 1 < have
            one = todo[slot, 2 * i]
            other = todo[slot, jnp.where(two, 2 * i + 1, 2 * i)]
            there = jnp.where(two, 1.0, 0.0).astype(BF16)
            query = mq_ref[slot]
            ones = jnp.ones((tile_size, lanes), BF16)
            for p in range(feature // lanes):
                part = slice(p * lanes, (p + 1) * lanes)
                key = jnp.concatenate([keys[one, :, part], keys[other, :, part]], axis=0)
                value = jnp.concatenate(
                    [
                        jnp.concatenate([values[one, :, part], ones], axis=1),
                        jnp.concatenate([values[other, :, part], ones], axis=1) * there,
                    ],
                    axis=0,
                )
                q = query[:, part]
                stacked = jnp.concatenate([jnp.where(first, q, zero), jnp.where(first, zero, q)], axis=0)
                weights = jnp.exp2(contract_last(stacked, key)).astype(BF16)
                both = jnp.dot(weights, value, preferred_element_type=F32)
                acc_ref[0, :, part] += jnp.where(first, both[:tile_size, :lanes], both[tile_size:, :lanes])
                acc_ref[1, :, part] += jnp.where(first, both[:tile_size, lanes:], both[tile_size:, lanes:])
            return carry

        lax.fori_loop(0, (have + 1) // 2, step, 0)
        if last:
            t = tile_of[slot]
            a, b = t // tile_cols, t % tile_cols
            half = tile_size // 2
            nums = [acc_ref[0, s * half : (s + 1) * half] for s in range(2)]
            dens = [acc_ref[1, s * half : (s + 1) * half] for s in range(2)]
            finish(a, b, nums, dens, tokens_ref, wo_ref, staged.at[slot])
            copy_of(slot).start()
        else:
            acc_out_ref[slot] = acc_ref[...]
        return carry

    def copy_of(slot):
        t = tile_of[slot]
        a, b = t // tile_cols, t % tile_cols
        return pltpu.make_async_copy(
            staged.at[slot],
            out_ref.at[
                pl.ds(a * TILE_ROWS, TILE_ROWS), pl.ds(pl.multiple_of(b * TILE_COLS, TILE_COLS), TILE_COLS)
            ],
            sems.at[slot],
        )

    lax.fori_loop(0, slots, attend, 0)
    if last:
        def drain(slot, carry):
            copy_of(slot).wait()
            return carry

        lax.fori_loop(0, slots, drain, 0)


def body(
    tokens,
    norm_gain,
    query_weight,
    key_weight,
    value_weight,
    out_weight,
    head_scale,
    counts,
    sources,
):
    grid_rows, grid_cols, feature = tokens.shape
    tile_rows = grid_rows // TILE_ROWS
    tile_cols = grid_cols // TILE_COLS
    tiles = tile_rows * tile_cols
    tile_size = TILE_ROWS * TILE_COLS
    keep = tiles - min(4, MASK_MOST)
    col_count = lax.axis_size("col")
    vmem = pl.BlockSpec(memory_space=pltpu.VMEM)
    smem = pl.BlockSpec(memory_space=pltpu.SMEM)
    hbm = pl.BlockSpec(memory_space=pl.ANY)

    free = jnp.repeat(jnp.repeat(counts == 0, TILE_ROWS, axis=0), TILE_COLS, axis=1)[..., None]
    mark = jnp.asarray(MARK, tokens.dtype)
    left = jnp.where(free[:, :RADIUS], tokens[:, :RADIUS], mark)
    right = jnp.where(free[:, -RADIUS:], tokens[:, -RADIUS:], mark)
    before, after = pair_swap(left, right, "col")
    gap = jnp.full((grid_rows, TILE_COLS - 2 * RADIUS, feature), mark)
    tail = jnp.concatenate([after, gap, before], axis=1)
    upper = jnp.concatenate([jnp.where(free[:RADIUS], tokens[:RADIUS], mark), tail[:RADIUS]], axis=1)
    lower = jnp.concatenate([jnp.where(free[-RADIUS:], tokens[-RADIUS:], mark), tail[-RADIUS:]], axis=1)
    top, bottom = pair_swap(upper, lower, "row")

    sizes = (keep - LATE_TILES, LATE_TILES)
    packed = pl.pallas_call(
        functools.partial(pack_kernel, tile_cols, keep),
        out_shape=[jax.ShapeDtypeStruct((n, tile_size, feature), tokens.dtype) for n in sizes],
        in_specs=[smem, vmem],
        out_specs=[vmem] * 2,
        name="pack",
    )(counts, tokens)
    rel_counts = spread(counts, "col")
    early = spread(packed[0], "col")
    late = spread(packed[1], "col")

    gain = norm_gain.reshape(1, feature)
    scale = jnp.repeat(head_scale * LOG2E, feature // HEADS).reshape(1, feature)
    acc_shape = jax.ShapeDtypeStruct((MASK_MOST, 2, tile_size, feature), F32)
    mq_shape = jax.ShapeDtypeStruct((MASK_MOST, tile_size, feature), BF16)
    padded = grid_rows + 2 * RADIUS
    lanes = 2 * feature // HEADS
    out, acc, mq = pl.pallas_call(
        near_kernel,
        out_shape=[jax.ShapeDtypeStruct(tokens.shape, tokens.dtype), acc_shape, mq_shape],
        in_specs=[smem] + [vmem] * 10,
        out_specs=[vmem] * 3,
        scratch_shapes=[
            pltpu.VMEM((2, padded, grid_cols, feature), BF16),
            pltpu.VMEM((2, padded, grid_cols, feature), BF16),
            pltpu.VMEM((2, padded, grid_cols, lanes), BF16),
            pltpu.VMEM((tile_rows, grid_cols // SIDE, TILE_ROWS * SIDE, feature), BF16),
            pltpu.VMEM((feature, feature), BF16),
        ],
        cost_estimate=pl.CostEstimate(flops=20_000_000_000, bytes_accessed=20_000_000, transcendentals=3_000_000),
        name="near",
    )(counts, tokens, tail, top, bottom, gain, scale, query_weight, key_weight, value_weight, out_weight)

    me = jnp.stack([lax.axis_index("col"), lax.axis_index("row")]).astype(jnp.int32)
    rels = sorted(rel_counts)
    slots = MASK_MOST * S_MAX

    def far(chunks, acc, last):
        plan = {"rels": rels, "chunks": [name for name, _ in chunks]}
        args = [me, counts, sources] + [rel_counts[r] for r in rels] + [item for _, item in chunks]
        specs = [smem] * (3 + len(rels)) + [vmem] * len(chunks)
        args += [mq, acc, gain, key_weight, value_weight]
        specs += [vmem] * 5
        scratch = [
            pltpu.VMEM((slots + 1, tile_size, feature), BF16),
            pltpu.VMEM((slots + 1, tile_size, feature), BF16),
            pltpu.VMEM((feature, feature), BF16),
            pltpu.VMEM((2, tile_size, feature), BF16),
            pltpu.VMEM((2, tile_size, feature), F32),
            pltpu.SMEM((slots,), jnp.int32),
            pltpu.SMEM((col_count * tiles,), jnp.int32),
            pltpu.SMEM((MASK_MOST, S_MAX), jnp.int32),
            pltpu.SMEM((MASK_MOST,), jnp.int32),
            pltpu.SMEM((MASK_MOST,), jnp.int32),
        ]
        if last:
            args += [tokens, out_weight, out]
            specs += [vmem, vmem, hbm]
            scratch += [
                pltpu.VMEM((MASK_MOST, TILE_ROWS, TILE_COLS, feature), BF16),
                pltpu.SemaphoreType.DMA((MASK_MOST,)),
            ]
        return pl.pallas_call(
            functools.partial(far_kernel, plan, last, tile_cols * col_count, None),
            out_shape=jax.ShapeDtypeStruct(out.shape, out.dtype) if last else acc_shape,
            in_specs=specs,
            out_specs=hbm if last else vmem,
            scratch_shapes=scratch,
            input_output_aliases={len(args) - 1: 0} if last else {},
            cost_estimate=pl.CostEstimate(flops=5_000_000_000, bytes_accessed=10_000_000, transcendentals=1_000_000),
            name="far_last" if last else "far",
        )(*args)

    acc = far([((r, 0, sizes[0]), early[r]) for r in rels], acc, False)
    return far([((r, sizes[0], sizes[1]), late[r]) for r in rels], acc, True)


def solution(mesh):
    placed = (
        P(("slab", "row"), "col", None),
        P(),
        P(),
        P(),
        P(),
        P(),
        P(),
        P(("slab", "row"), "col"),
        P(("slab", "row"), "col", None),
    )
    return jax.shard_map(
        body, mesh=mesh, in_specs=placed, out_specs=P(("slab", "row"), "col", None), check_vma=False
    )
```

time: 634 us -> 111 us (0.18); the launches traced: 622 us -> 110 us
  local copies, waits for them, and re-layouts: 281 us -> 4.29 us
  matrix products: 254 us -> 0 us
  Pallas kernels: 0 us -> 73.9 us
  starting transfers between devices: 49.6 us -> 24.5 us
  other arithmetic: 21.7 us -> 4.09 us
  loops' own time: 10.6 us -> 0 us
    dot_general x25 -> x0, matrix products: 254 us -> none  [the longest x8 102 us: near_row(): jnp.einsum('bhrcsk,sbkhd->rbchd', weights.astype(jnp.bfloat16), value_par...]
    gather x2 -> x0, local copies, waits for them, and re-layouts: 89.4 us -> none  [pick_tiles(): picked = source_grid[row_pick, col_pick]]
    pallas_call x0 -> x4, Pallas kernels: none -> 73.9 us  [the longest x2 38 us: far(): pl.pallas_call(functools.partial(far_kernel, plan, last, tile_cols * col_...]
    reshape x24 -> x2, local copies, waits for them, and re-layouts: 71.9 us -> 0.63 us  [the longest x1 0.54 us: body(): gain = norm_gain.reshape(1, feature)]
    slice x14 -> x4, local copies, waits for them, and re-layouts: 49.4 us -> 0.3 us  [the longest x2 0.18 us: body(): free[:RADIUS]]
    convert_element_type x5 -> x0, local copies, waits for them, and re-layouts: 24.9 us -> none  [the longest x4 20.6 us: unit_heads(): return (split_heads * inverse_len * head_factor[:, None]).reshape(project...]
    convert_element_type x7 -> x0, other arithmetic: 14.9 us -> none  [the longest x1 7.7 us: body(): (numerator / denominator[..., None]).astype(jnp.bfloat16)]
    all_to_all x3 -> x0, starting transfers between devices: 12.7 us -> none  [the longest x1 4.81 us: body(): lax.all_to_all(pick_tiles(halo_keys, source_offset, wanted, tile_cols), '...]
  transfers between devices with their start and end apart: 11 -> 13, of which waited for: 3 -> 2; matrix products, arithmetic and copies ran while one was open for 79% -> 6% of each run, Pallas kernels for 0% -> 53%
where the time goes in v1:
time: 111 us; the launch traced here: 110 us
  Pallas kernels  73.9 us (67%)
  starting transfers between devices  24.5 us (22%)
  local copies, waits for them, and re-layouts  4.29 us (4%)
  other arithmetic  4.09 us (4%)
  waiting for transfers between devices  2.97 us (3%)
    pallas_call x2, Pallas kernels, far(): pl.pallas_call(functools.partial(far_kernel, plan, last, tile_cols * col_...  38 us
    pallas_call x1, Pallas kernels, body(): pl.pallas_call(near_kernel, out_shape=[jax.ShapeDtypeStruct(tokens.shape,...  33.1 us
    ppermute x9, starting transfers between devices, spread(): lax.ppermute(item, axis, pairs)  20 us
    ppermute x2, starting transfers between devices, pair_swap(): two = lax.ppermute(jnp.where(even, low, high), axis, both(second))  4.14 us
    pallas_call x1, Pallas kernels, body(): pl.pallas_call(functools.partial(pack_kernel, tile_cols, keep), out_shape...  2.81 us
  transfers between devices with their start and end apart: 13, of which 2 were waited for; matrix products, arithmetic and copies ran while one was open for 6% of the time, Pallas kernels for 53%

profile of v1, /device:TPU:8, one launch (start us, length us, event | category | flops | bytes accessed | tf_op | source)
XLA Modules:
  0.0 110.0 jit_solution(1870537697984514966)
XLA Ops:
  0.0 2.8 %pack.1 = (bf16[8,128,384]{2,1,0:T(8,128)(2,1)}, bf16[4,128,384]{2,1,0:T(8,128)(2,1)}) custom-call(s32[4,4]{1,0:T(4,128)} %refs_3_.3, bf16[32,64,384]{2,1,0:T(8,128)(2,1)} %refs_16_.1), custom_call_target="tpu_custom_call" | custom-call | tf_op jit(solution)/shard_map/pack/pallas_call | solution.py:422
  2.8 1.6 %collective-permute-start.11 = (bf16[8,128,384]{2,1,0:T(8,128)(2,1)}, bf16[8,128,384]{2,1,0:T(8,128)(2,1)S(1)}, u32[]{:S(2)}, u32[]{:S(2)}) collective-permute-start(bf16[8,128,384]{2,1,0:T(8,128)(2,1)} %get-tuple-element.12.refs_7_), channel_id=1, source_target_pairs={{0,8},{4,12},{8,0},{12,4},{1,9},{5,13},{9,1},{13,5},{2,10},{6,14},... | collective-permute-start | bytes 2359304 | tf_op jit(solution)/shard_map/ppermute | solution.py:46
  4.4 0.0 collective-permute-start.10
  4.4 0.0 copy-done.1
  4.4 0.5 collective-permute-start.1
  4.9 0.1 copy.11
  5.0 0.1 broadcast_in_dim.69
  5.1 0.1 reshape.10
  5.2 0.1 copy.12
  5.3 0.1 copy.13
  5.4 1.2 %broadcast_select_fusion.3 = (bf16[32,3,384]{2,1,0:T(4,128)(2,1)S(1)}, bf16[32,3,384]{2,1,0:T(4,128)(2,1)S(1)}) fusion(pred[]{:T(512)S(6)} %eq.25, bf16[32,64,384]{2,1,0:T(8,128)(2,1)} %refs_16_.1, pred[32,3]{1,0:T(8,128)(4,1)S(1)} %copy.12, pred[32,3]{1,0:T(8,128)(4,1)S(1)} %copy.13), kind=kLoop, calls=%fused_computation.14 | loop fusion | flops 147456 | bytes 295105 | tf_op jit(solution)/shard_map/jit(_where)/select_n | solution.py:32
  6.7 0.3 collective-permute-start.6
  7.0 0.7 collective-permute-start.7
  7.6 0.1 fusion.1
  7.7 0.1 copy.14
  7.8 0.1 broadcast_in_dim.77
  7.9 0.1 broadcast_in_dim.78
  8.0 0.1 copy.15
  8.1 0.1 broadcast_in_dim.81
  8.2 0.1 broadcast_in_dim.82
  8.2 1.1 %slice_select_fusion.1 = (bf16[3,64,384]{2,1,0:T(8,128)(2,1)S(1)}, bf16[3,64,384]{2,1,0:T(8,128)(2,1)S(1)}) fusion(bf16[32,64,384]{2,1,0:T(8,128)(2,1)} %refs_16_.1, pred[3,64]{1,0:T(4,128)(4,1)S(1)} %broadcast_in_dim.78, pred[3,64]{1,0:T(4,128)(4,1)S(1)} %broadcast_in_dim.82), kind=kLoop, calls=%fused_computation.8 | loop fusion | flops 147456 | bytes 590208 | tf_op jit(solution)/shard_map/jit(_where)/select_n | solution.py:417
  9.4 0.1 pad.5.clone
  9.5 0.0 collective-permute-done.6
  9.5 0.0 collective-permute-done.7
  9.5 0.1 select_select_fusion.3
  9.6 0.2 pad_maximum_fusion.tail_ref
  9.7 0.0 copy-start
  9.8 0.1 broadcast_select_fusion
  9.8 3.5 %collective-permute-start.8 = (bf16[3,80,384]{2,1,0:T(8,128)(2,1)S(1)}, bf16[3,80,384]{2,1,0:T(8,128)(2,1)S(1)}, u32[]{:S(2)}, u32[]{:S(2)}) collective-permute-start(bf16[3,80,384]{2,1,0:T(8,128)(2,1)S(1)} %get-tuple-element.24), channel_id=1, source_target_pairs={{1,2},{2,1},{5,6},{6,5},{9,10},{10,9},{13,14},{14,13},{17,18},{18,... | collective-permute-start | bytes 552968 | tf_op jit(solution)/shard_map/ppermute | solution.py:33
  13.3 0.1 collective-permute-start.9
  13.4 0.0 copy-done.11
  13.4 0.0 copy-done.2
  13.5 0.5 reshape.11.gain_ref.refs_13_
  14.0 0.1 broadcast_in_dim.84
  14.1 0.7 reshape_reshape.3.scale_ref
  14.7 0.6 pad_add_fusion.refs_0_
  15.3 2.0 %collective-permute-done.8 = bf16[3,80,384]{2,1,0:T(8,128)(2,1)S(1)} collective-permute-done((bf16[3,80,384]{2,1,0:T(8,128)(2,1)S(1)}, bf16[3,80,384]{2,1,0:T(8,128)(2,1)S(1)}, u32[]{:S(2)}, u32[]{:S(2)}) %collective-permute-start.8) | collective-permute-done | bytes 184352 | tf_op jit(solution)/shard_map/ppermute | solution.py:33
  17.3 12.7 %collective-permute-start = (s32[4,4]{1,0:T(4,128)S(1)}, s32[4,4]{1,0:T(4,128)S(1)}, u32[]{:S(2)}, u32[]{:S(2)}) collective-permute-start(s32[4,4]{1,0:T(4,128)S(1)} %copy-done.1), channel_id=1, source_target_pairs={{0,4},{4,0},{8,12},{12,8},{1,5},{5,1},{9,13},{13,9},{2,6},{6,2},{1... | collective-permute-start | bytes 200 | tf_op jit(solution)/shard_map/ppermute | solution.py:46
  30.0 0.0 collective-permute-done.9
  30.0 0.0 copy-done.5
  30.0 4.4 %collective-permute-start.4 = (bf16[4,128,384]{2,1,0:T(8,128)(2,1)S(1)}, bf16[4,128,384]{2,1,0:T(8,128)(2,1)}, u32[]{:S(2)}, u32[]{:S(2)}) collective-permute-start(bf16[4,128,384]{2,1,0:T(8,128)(2,1)S(1)} %copy-done.5), channel_id=1, source_target_pairs={{0,8},{4,12},{8,0},{12,4},{1,9},{5,13},{9,1},{13,5},{2,10},{6,14},... | collective-permute-start | bytes 1179656 | tf_op jit(solution)/shard_map/ppermute | solution.py:46
  34.4 0.8 select_select_fusion
  35.2 0.0 collective-permute-done.11.refs_9_
  35.2 0.0 collective-permute-start.12
  35.2 0.0 copy-done
  35.2 33.1 %near.1 = (bf16[32,64,384]{2,1,0:T(8,128)(2,1)}, f32[8,2,128,384]{3,2,1,0:T(8,128)}, bf16[8,128,384]{2,1,0:T(8,128)(2,1)}) custom-call(s32[4,4]{1,0:T(4,128)} %refs_3_.3, bf16[32,64,384]{2,1,0:T(8,128)(2,1)} %refs_16_.1, bf16[32,16,384]{2,1,0:T(8,128)(2,1)} %copy-done, bf16[3,80,384]{2,1,0:T(8,128)(2,1)} %get-tuple-element.22.top_ref, ...), custom_call_target="tpu_custom_call" | custom-call | flops 20000000000 | bytes 20000000 | tf_op jit(solution)/shard_map/near/pallas_call | solution.py:439
  68.3 0.0 collective-permute-done.1.refs_5_
  68.3 0.3 collective-permute-start.3
  68.6 0.0 collective-permute-done.refs_4_
  68.6 0.3 collective-permute-start.2
  68.9 0.0 collective-permute-done.4.refs_9_
  68.9 0.2 collective-permute-start.5
  69.1 1.0 collective-permute-done.2.refs_6_
  70.1 0.0 collective-permute-done.10.refs_8_
  70.1 0.0 collective-permute-done.12.refs_10_
  70.1 0.5 copy-done.10
  70.7 0.3 copy-done.4
  71.0 25.1 %far.1.refs_12_ = f32[8,2,128,384]{3,2,1,0:T(8,128)} custom-call(s32[2]{0:T(128)} %pad_add_fusion.refs_0_, s32[4,4]{1,0:T(4,128)} %refs_3_.3, s32[4,4,4]{2,1,0:T(4,128)} %refs_2_.3, s32[4,4]{1,0:T(4,128)} %refs_3_.3, s32[4,4]{1,0:T(4,128)} %copy-done.9, s32[4,4]{1,0:T(4,128)} %copy-done.8, s32[4,4]{1,0:T(4,128)} %copy-done.10, ...), custom_call_target="tpu_custom_call" | custom-call | flops 5000000000 | bytes 10000000 | tf_op jit(solution)/shard_map/far/pallas_call | solution.py:484
  96.1 0.0 collective-permute-done.3.refs_8_
  96.1 0.0 collective-permute-done.5.refs_10_
  96.1 0.0 copy-start.7
  96.2 0.8 copy-done.6
  96.9 0.1 copy-done.7
  97.1 12.9 %far_last.1 = bf16[32,64,384]{2,1,0:T(8,128)(2,1)} custom-call(s32[2]{0:T(128)} %pad_add_fusion.refs_0_, s32[4,4]{1,0:T(4,128)} %refs_3_.3, s32[4,4,4]{2,1,0:T(4,128)} %refs_2_.3, s32[4,4]{1,0:T(4,128)} %refs_3_.3, s32[4,4]{1,0:T(4,128)} %copy-done.9, s32[4,4]{1,0:T(4,128)} %copy-done.8, s32[4,4]{1,0:T(4,128)} %copy-done.10, ...), custom_call_target="tpu_custom_call", output_to_operand_aliasing={{}: (18, {})} | custom-call | flops 5000000000 | bytes 10000000 | tf_op jit(solution)/shard_map/far_last/pallas_call | solution.py:484
  (19 shorter events, 0.1 us)
Async XLA Ops:
  0.0 4.4 %copy-start.1 = (s32[4,4]{1,0:T(4,128)S(1)}, s32[4,4]{1,0:T(4,128)}, u32[]{:S(2)}) copy-start(s32[4,4]{1,0:T(4,128)} %refs_3_.3) | copy-start | bytes 196
  2.8 10.6 %copy-start.11 = (f32[6]{0:T(128)S(1)}, f32[6]{0:T(128)}, u32[]{:S(2)}) copy-start(f32[6]{0:T(128)} %param.15) | copy-start | bytes 76
  2.8 10.6 %copy-start.2 = (f32[384]{0:T(512)S(1)}, f32[384]{0:T(512)}, u32[]{:S(2)}) copy-start(f32[384]{0:T(512)} %param.10) | copy-start | bytes 4612
  2.8 27.1 %copy-start.5 = (bf16[4,128,384]{2,1,0:T(8,128)(2,1)S(1)}, bf16[4,128,384]{2,1,0:T(8,128)(2,1)}, u32[]{:S(2)}) copy-start(bf16[4,128,384]{2,1,0:T(8,128)(2,1)} %get-tuple-element.10.refs_7_) | copy-start | bytes 1179652
  2.8 32.3 %collective-permute-start.11 = (bf16[8,128,384]{2,1,0:T(8,128)(2,1)}, bf16[8,128,384]{2,1,0:T(8,128)(2,1)S(1)}, u32[]{:S(2)}, u32[]{:S(2)}) collective-permute-start(bf16[8,128,384]{2,1,0:T(8,128)(2,1)} %get-tuple-element.12.refs_7_), channel_id=1, source_target_pairs={{0,8},{4,12},{8,0},{12,4},{1,9},{5,13},{9,1},{13,5},{2,10},{6,14},... | collective-permute-start | bytes 2359304 | tf_op jit(solution)/shard_map/ppermute | solution.py:46
  4.4 65.7 %collective-permute-start.10 = (bf16[8,128,384]{2,1,0:T(8,128)(2,1)}, bf16[8,128,384]{2,1,0:T(8,128)(2,1)S(1)}, u32[]{:S(2)}, u32[]{:S(2)}) collective-permute-start(bf16[8,128,384]{2,1,0:T(8,128)(2,1)} %get-tuple-element.12.refs_7_), channel_id=1, source_target_pairs={{0,4},{4,0},{8,12},{12,8},{1,5},{5,1},{9,13},{13,9},{2,6},{6,2},{1... | collective-permute-start | bytes 2359304 | tf_op jit(solution)/shard_map/ppermute | solution.py:46
  4.4 63.9 %collective-permute-start.1 = (s32[4,4]{1,0:T(4,128)S(1)}, s32[4,4]{1,0:T(4,128)S(1)}, u32[]{:S(2)}, u32[]{:S(2)}) collective-permute-start(s32[4,4]{1,0:T(4,128)S(1)} %copy-done.1), channel_id=1, source_target_pairs={{0,8},{4,12},{8,0},{12,4},{1,9},{5,13},{9,1},{13,5},{2,10},{6,14},... | collective-permute-start | bytes 200 | tf_op jit(solution)/shard_map/ppermute | solution.py:46
  6.7 2.8 %collective-permute-start.6 = (bf16[32,3,384]{2,1,0:T(4,128)(2,1)S(1)}, bf16[32,3,384]{2,1,0:T(4,128)(2,1)S(1)}, u32[]{:S(2)}, u32[]{:S(2)}) collective-permute-start(bf16[32,3,384]{2,1,0:T(4,128)(2,1)S(1)} %get-tuple-element.15), channel_id=1, source_target_pairs={{0,4},{8,12},{4,0},{12,8},{1,5},{9,13},{5,1},{13,9},{2,6},{10,14},... | collective-permute-start | bytes 221192 | tf_op jit(solution)/shard_map/ppermute | solution.py:32
  7.0 2.5 %collective-permute-start.7 = (bf16[32,3,384]{2,1,0:T(4,128)(2,1)S(1)}, bf16[32,3,384]{2,1,0:T(4,128)(2,1)S(1)}, u32[]{:S(2)}, u32[]{:S(2)}) collective-permute-start(bf16[32,3,384]{2,1,0:T(4,128)(2,1)S(1)} %get-tuple-element.16), channel_id=1, source_target_pairs={{4,8},{8,4},{5,9},{9,5},{6,10},{10,6},{7,11},{11,7},{20,24},{24,20... | collective-permute-start | bytes 221192 | tf_op jit(solution)/shard_map/ppermute | solution.py:33
  9.7 25.4 %copy-start = (bf16[32,16,384]{2,1,0:T(8,128)(2,1)}, bf16[32,16,384]{2,1,0:T(8,128)(2,1)S(1)}, u32[]{:S(2)}) copy-start(bf16[32,16,384]{2,1,0:T(8,128)(2,1)S(1)} %pad_maximum_fusion.tail_ref) | copy-start | bytes 1179652
  9.8 7.4 %collective-permute-start.8 = (bf16[3,80,384]{2,1,0:T(8,128)(2,1)S(1)}, bf16[3,80,384]{2,1,0:T(8,128)(2,1)S(1)}, u32[]{:S(2)}, u32[]{:S(2)}) collective-permute-start(bf16[3,80,384]{2,1,0:T(8,128)(2,1)S(1)} %get-tuple-element.24), channel_id=1, source_target_pairs={{1,2},{2,1},{5,6},{6,5},{9,10},{10,9},{13,14},{14,13},{17,18},{18,... | collective-permute-start | bytes 552968 | tf_op jit(solution)/shard_map/ppermute | solution.py:33
  13.3 16.6 %collective-permute-start.9 = (bf16[3,80,384]{2,1,0:T(8,128)(2,1)S(1)}, bf16[3,80,384]{2,1,0:T(8,128)(2,1)S(1)}, u32[]{:S(2)}, u32[]{:S(2)}) collective-permute-start(bf16[3,80,384]{2,1,0:T(8,128)(2,1)S(1)} %get-tuple-element.23), channel_id=1, source_target_pairs={{0,1},{2,3},{1,0},{3,2},{4,5},{6,7},{5,4},{7,6},{8,9},{10,11},{9,8... | collective-permute-start | bytes 552968 | tf_op jit(solution)/shard_map/ppermute | solution.py:32
  17.3 51.3 %collective-permute-start = (s32[4,4]{1,0:T(4,128)S(1)}, s32[4,4]{1,0:T(4,128)S(1)}, u32[]{:S(2)}, u32[]{:S(2)}) collective-permute-start(s32[4,4]{1,0:T(4,128)S(1)} %copy-done.1), channel_id=1, source_target_pairs={{0,4},{4,0},{8,12},{12,8},{1,5},{5,1},{9,13},{13,9},{2,6},{6,2},{1... | collective-permute-start | bytes 200 | tf_op jit(solution)/shard_map/ppermute | solution.py:46
  30.0 38.9 %collective-permute-start.4 = (bf16[4,128,384]{2,1,0:T(8,128)(2,1)S(1)}, bf16[4,128,384]{2,1,0:T(8,128)(2,1)}, u32[]{:S(2)}, u32[]{:S(2)}) collective-permute-start(bf16[4,128,384]{2,1,0:T(8,128)(2,1)S(1)} %copy-done.5), channel_id=1, source_target_pairs={{0,8},{4,12},{8,0},{12,4},{1,9},{5,13},{9,1},{13,5},{2,10},{6,14},... | collective-permute-start | bytes 1179656 | tf_op jit(solution)/shard_map/ppermute | solution.py:46
  35.2 33.1 %copy-start.3 = (bf16[8,128,384]{2,1,0:T(8,128)(2,1)}, bf16[8,128,384]{2,1,0:T(8,128)(2,1)S(1)}, u32[]{:S(2)}) copy-start(bf16[8,128,384]{2,1,0:T(8,128)(2,1)S(1)} %collective-permute-done.11.refs_9_) | copy-start | bytes 2359300
  35.2 34.9 %collective-permute-start.12 = (bf16[8,128,384]{2,1,0:T(8,128)(2,1)S(1)}, bf16[8,128,384]{2,1,0:T(8,128)(2,1)}, u32[]{:S(2)}, u32[]{:S(2)}) collective-permute-start(bf16[8,128,384]{2,1,0:T(8,128)(2,1)S(1)} %collective-permute-done.11.refs_9_), channel_id=1, source_target_pairs={{0,4},{4,0},{8,12},{12,8},{1,5},{5,1},{9,13},{13,9},{2,6},{6,2},{1... | collective-permute-start | bytes 2359304 | tf_op jit(solution)/shard_map/ppermute | solution.py:46
  68.3 1.8 %copy-start.8 = (s32[4,4]{1,0:T(4,128)}, s32[4,4]{1,0:T(4,128)S(1)}, u32[]{:S(2)}) copy-start(s32[4,4]{1,0:T(4,128)S(1)} %collective-permute-done.1.refs_5_) | copy-start | bytes 196
  68.3 27.8 %collective-permute-start.3 = (bf16[4,128,384]{2,1,0:T(8,128)(2,1)S(1)}, bf16[4,128,384]{2,1,0:T(8,128)(2,1)S(1)}, u32[]{:S(2)}, u32[]{:S(2)}) collective-permute-start(bf16[4,128,384]{2,1,0:T(8,128)(2,1)S(1)} %copy-done.5), channel_id=1, source_target_pairs={{0,4},{4,0},{8,12},{12,8},{1,5},{5,1},{9,13},{13,9},{2,6},{6,2},{1... | collective-permute-start | bytes 1179656 | tf_op jit(solution)/shard_map/ppermute | solution.py:46
  68.6 1.5 %copy-start.9 = (s32[4,4]{1,0:T(4,128)}, s32[4,4]{1,0:T(4,128)S(1)}, u32[]{:S(2)}) copy-start(s32[4,4]{1,0:T(4,128)S(1)} %collective-permute-done.refs_4_) | copy-start | bytes 196
  68.6 1.5 %collective-permute-start.2 = (s32[4,4]{1,0:T(4,128)S(1)}, s32[4,4]{1,0:T(4,128)S(1)}, u32[]{:S(2)}, u32[]{:S(2)}) collective-permute-start(s32[4,4]{1,0:T(4,128)S(1)} %collective-permute-done.1.refs_5_), channel_id=1, source_target_pairs={{0,4},{4,0},{8,12},{12,8},{1,5},{5,1},{9,13},{13,9},{2,6},{6,2},{1... | collective-permute-start | bytes 200 | tf_op jit(solution)/shard_map/ppermute | solution.py:46
  68.9 27.2 %collective-permute-start.5 = (bf16[4,128,384]{2,1,0:T(8,128)(2,1)}, bf16[4,128,384]{2,1,0:T(8,128)(2,1)S(1)}, u32[]{:S(2)}, u32[]{:S(2)}) collective-permute-start(bf16[4,128,384]{2,1,0:T(8,128)(2,1)} %collective-permute-done.4.refs_9_), channel_id=1, source_target_pairs={{0,4},{4,0},{8,12},{12,8},{1,5},{5,1},{9,13},{13,9},{2,6},{6,2},{1... | collective-permute-start | bytes 1179656 | tf_op jit(solution)/shard_map/ppermute | solution.py:46
  70.1 0.6 copy-start.10
  70.1 0.9 copy-start.4
  96.1 0.8 copy-start.6
  96.1 0.9 copy-start.7

commit v2 on v1

v2 whole, which is shorter than its diff:
```python
import functools
import math
import jax
import jax.numpy as jnp
from jax import lax
from jax.experimental import pallas as pl
from jax.experimental.pallas import tpu as pltpu
from jax.sharding import PartitionSpec as P

HEADS = 6
TILE_ROWS = 8
TILE_COLS = 16
RADIUS = 3
S_MAX = 4
MASK_MOST = 8
SIDE = 8
MARK = 1024.0
MARK_LEVEL = 1000.0
LATE_TILES = 4
GAP = 2
LOG2E = math.log2(math.e)
F32 = jnp.float32
BF16 = jnp.bfloat16


def pair_swap(low, high, axis):
    count = lax.axis_size(axis)
    index = lax.axis_index(axis)
    even = index % 2 == 0
    first = [(i, i + 1) for i in range(0, count - 1, 2)]
    second = [(i, i + 1) for i in range(1, count - 1, 2)]
    both = lambda pairs: pairs + [(b, a) for a, b in pairs]
    one = lax.ppermute(jnp.where(even, high, low), axis, both(first))
    two = lax.ppermute(jnp.where(even, low, high), axis, both(second))
    mark = jnp.asarray(MARK, low.dtype)
    before = jnp.where(index == 0, mark, jnp.where(even, two, one))
    after = jnp.where(index == count - 1, mark, jnp.where(even, one, two))
    return before, after


def spread(array, axis):
    count = lax.axis_size(axis)
    held = {0: array}
    bit = count // 2
    while bit:
        pairs = [(i, i ^ bit) for i in range(count)]
        held.update({rel ^ bit: lax.ppermute(item, axis, pairs) for rel, item in held.items()})
        bit //= 2
    return held


def pack_kernel(tile_cols, counts_ref, tokens_ref, *chunk_refs):
    tile_rows = tokens_ref.shape[0] // TILE_ROWS
    free = jnp.int32(0)
    for t in range(tile_rows * tile_cols):
        free = free + (counts_ref[t // tile_cols, t % tile_cols] == 0).astype(jnp.int32)
    seen_free = jnp.int32(0)
    seen_masked = jnp.int32(0)
    for t in range(tile_rows * tile_cols):
        a, b = t // tile_cols, t % tile_cols
        is_free = (counts_ref[a, b] == 0).astype(jnp.int32)
        rank = jnp.where(is_free == 1, seen_free, free + seen_masked)
        seen_free = seen_free + is_free
        seen_masked = seen_masked + 1 - is_free
        low = 0
        for ref in chunk_refs:
            size = ref.shape[0]

            @pl.when((rank >= low) & (rank < low + size))
            def _(ref=ref, low=low, a=a, b=b, rank=rank):
                ref[rank - low] = tokens_ref[
                    TILE_ROWS * a : TILE_ROWS * (a + 1), TILE_COLS * b : TILE_COLS * (b + 1), :
                ].reshape(TILE_ROWS * TILE_COLS, tokens_ref.shape[-1])

            low += size


def split_by(value, size):
    if size & (size - 1) == 0:
        return value >> (size.bit_length() - 1), value & (size - 1)
    return value // size, value % size


def plan_kernel(rels, all_cols, early_size, counts_ref, sources_ref, *refs):
    rel_counts = refs[: len(rels)]
    needed, totals, todo, todo_count, tile_of, place, ranks = refs[len(rels) :]
    tile_rows, tile_cols = counts_ref.shape
    tiles = tile_rows * tile_cols
    my_col = lax.axis_index("col")
    my_band = lax.axis_index("row")
    for rel, ref in zip(rels, rel_counts):
        rank = jnp.int32(0)
        for t in range(tiles):
            ranks[rel * tiles + t] = rank
            place[rel * tiles + t] = -1
            rank = rank + (ref[t // tile_cols, t % tile_cols] == 0).astype(jnp.int32)
    for slot in range(MASK_MOST):
        todo_count[0, slot] = 0
        todo_count[1, slot] = 0
    totals[0] = 0
    totals[1] = 0

    def plan_tile(t, slot):
        a, b = split_by(t, tile_cols)
        live = counts_ref[a, b]
        tile_of[jnp.where(live > 0, slot, MASK_MOST)] = t

        def plan_entry(j, carry):
            row, col = split_by(sources_ref[a, b, j], all_cols)
            owner, sb = split_by(col, tile_cols)
            where = (owner ^ my_col) * tiles
            rank = ranks[where + (row - my_band * tile_rows) * tile_cols + sb]
            name = where + rank
            phase = (rank >= early_size).astype(jnp.int32)
            at = place[name]
            count = totals[phase]
            fresh = at < 0
            at = jnp.where(fresh, count, at)
            place[name] = at
            needed[phase, at] = name
            totals[phase] = count + fresh.astype(jnp.int32)
            n = todo_count[phase, slot]
            todo[phase, slot, n] = at
            todo_count[phase, slot] = n + 1
            return carry

        lax.fori_loop(0, live, plan_entry, 0)
        return slot + (live > 0).astype(jnp.int32)

    totals[2] = lax.fori_loop(0, tiles, plan_tile, jnp.int32(0))


def unit(projected):
    feature = projected.shape[-1]
    lanes = 2 * feature // HEADS
    low = lax.broadcasted_iota(jnp.int32, (projected.shape[0], lanes), 1) < lanes // 2
    parts = []
    for p in range(feature // lanes):
        part = projected[:, p * lanes : (p + 1) * lanes]
        square = part * part
        first = jnp.sum(jnp.where(low, square, 0.0), axis=-1, keepdims=True)
        second = jnp.sum(jnp.where(low, 0.0, square), axis=-1, keepdims=True)
        parts.append(part * lax.rsqrt(jnp.where(low, first, second) + 1e-6))
    return jnp.concatenate(parts, axis=-1)


def normed_of(raw, gain):
    level = jnp.mean(raw * raw, axis=-1, keepdims=True)
    return raw * lax.rsqrt(level + 1e-6) * gain, level


def contract_last(left, right):
    return lax.dot_general(left, right, (((1,), (1,)), ((), ())), preferred_element_type=F32)


def near_kernel(
    scale_ref, counts_ref, tokens_ref, tail_ref, top_ref, bottom_ref, gain_ref,
    wq_ref, wk_ref, wv_ref, wo_ref,
    out_ref, acc_ref, mq_ref,
    keys, values, valid, queries, attended, wkv,
):
    grid_rows, grid_cols, feature = tokens_ref.shape
    tile_rows = grid_rows // TILE_ROWS
    tile_cols = grid_cols // TILE_COLS
    wide = tail_ref.shape[1] + grid_cols
    lanes = 2 * feature // HEADS
    win_rows = TILE_ROWS + 2 * RADIUS
    gain = gain_ref[...].reshape(1, feature)
    wkv[:, :feature] = wk_ref[...]
    wkv[:, feature:] = wv_ref[...]
    head = lax.broadcasted_iota(jnp.int32, (1, feature), 1) // (feature // HEADS)
    scale = jnp.zeros((1, feature), F32)
    for h in range(HEADS):
        scale = jnp.where(head == h, scale_ref[h] * LOG2E, scale)

    def put_keys(raw, own_valid, places):
        rows = raw.shape[0]
        normed, level = normed_of(raw, gain[None])
        ok = jnp.where(level < MARK_LEVEL, own_valid, 0.0)
        ok = pltpu.roll(jnp.broadcast_to(ok, (rows, wide, lanes)), RADIUS, 1)
        shifted = pltpu.roll(normed, RADIUS, 1).reshape(rows * wide, feature).astype(BF16)
        both = jnp.dot(shifted, wkv[...], preferred_element_type=F32)
        key = unit(both[:, :feature]).reshape(rows, wide, feature)
        value = both[:, feature:].reshape(rows, wide, feature)
        value = value * jnp.concatenate([ok] * (feature // lanes), axis=-1)
        for side in range(2):
            low = side * SIDE
            for at, start, size in places:
                into = (side, pl.ds(at, size))
                keys[into] = key[start : start + size, low : low + grid_cols].astype(BF16)
                values[into] = value[start : start + size, low : low + grid_cols].astype(BF16)
                valid[into] = ok[start : start + size, low : low + grid_cols].astype(BF16)
        return normed

    edge = jnp.concatenate([top_ref[...], bottom_ref[...]], axis=0).astype(F32)
    put_keys(edge, 1.0, ((0, 0, RADIUS), (RADIUS + grid_rows, RADIUS, RADIUS)))

    def project(a, carry):
        rows = pl.ds(a * TILE_ROWS, TILE_ROWS)
        raw = jnp.concatenate([tokens_ref[rows].astype(F32), tail_ref[rows].astype(F32)], axis=1)
        tile = lax.broadcasted_iota(jnp.int32, (1, wide, 1), 1) // TILE_COLS
        own_valid = jnp.ones((1, wide, 1), F32)
        for b in range(tile_cols):
            flag = jnp.where(counts_ref[a, b] == 0, 1.0, 0.0)
            own_valid = jnp.where(tile == b, flag, own_valid)
        normed = put_keys(raw, own_valid, ((RADIUS + a * TILE_ROWS, 0, TILE_ROWS),))
        flat = normed[:, :grid_cols].astype(BF16).reshape(TILE_ROWS * grid_cols, feature)
        query = unit(jnp.dot(flat, wq_ref[...], preferred_element_type=F32)) * scale
        query = query.reshape(TILE_ROWS, grid_cols // SIDE, SIDE, feature)
        for c in range(grid_cols // SIDE):
            queries[a, c] = query[:, c].reshape(TILE_ROWS * SIDE, feature).astype(BF16)
        return carry

    lax.fori_loop(0, tile_rows, project, 0)

    tokens_of_side = TILE_ROWS * SIDE
    window = win_rows * TILE_COLS
    qpos = lax.broadcasted_iota(jnp.int32, (2 * tokens_of_side, window), 0) % tokens_of_side
    kpos = lax.broadcasted_iota(jnp.int32, (2 * tokens_of_side, window), 1)
    down = kpos // TILE_COLS - qpos // SIDE
    across = kpos % TILE_COLS - qpos % SIDE
    inside = (down >= 0) & (down <= 2 * RADIUS) & (across >= 0) & (across <= 2 * RADIUS)
    band = jnp.where(inside, 1.0, 0.0).astype(BF16)
    first = lax.broadcasted_iota(jnp.int32, (tokens_of_side, lanes), 1) < lanes // 2
    zero = jnp.zeros((tokens_of_side, lanes), BF16)

    def attend(a, slot):
        for b in range(tile_cols):
            masked = counts_ref[a, b] > 0
            into = jnp.where(masked, slot, MASK_MOST)
            slot = slot + masked.astype(jnp.int32)
            for p in range(feature // lanes):
                part = slice(p * lanes, (p + 1) * lanes)
                sides = []
                for side in range(2):
                    at = (side, pl.ds(a * TILE_ROWS, win_rows), slice(b * TILE_COLS, (b + 1) * TILE_COLS))
                    ok = valid[at].reshape(window, lanes)
                    key = keys[(*at, part)].reshape(window, lanes)
                    value = jnp.concatenate([values[(*at, part)].reshape(window, lanes), ok], axis=1)
                    q = queries[a, 2 * b + side, :, part]
                    stacked = jnp.concatenate([jnp.where(first, q, zero), jnp.where(first, zero, q)], axis=0)
                    weights = jnp.exp2(contract_last(stacked, key)).astype(BF16) * band
                    both = jnp.dot(weights, value, preferred_element_type=F32)
                    num = jnp.where(first, both[:tokens_of_side, :lanes], both[tokens_of_side:, :lanes])
                    den = jnp.where(first, both[:tokens_of_side, lanes:], both[tokens_of_side:, lanes:])
                    rows = slice(side * tokens_of_side, (side + 1) * tokens_of_side)
                    acc_ref[into, 0, rows, part] = num
                    acc_ref[into, 1, rows, part] = den
                    mq_ref[into, rows, part] = q
                    den = jnp.where(masked, 1.0, den)
                    sides.append((num / den).reshape(TILE_ROWS, SIDE, lanes))
                attended[
                    pl.ds(a * TILE_ROWS, TILE_ROWS), b * TILE_COLS : (b + 1) * TILE_COLS, part
                ] = jnp.concatenate(sides, axis=1).astype(BF16)
        return slot

    lax.fori_loop(0, tile_rows, attend, jnp.int32(0))

    def finish(a, carry):
        rows = pl.ds(a * TILE_ROWS, TILE_ROWS)
        flat = attended[rows].reshape(TILE_ROWS * grid_cols, feature)
        raw = tokens_ref[rows].reshape(TILE_ROWS * grid_cols, feature).astype(F32)
        mixed = raw + jnp.dot(flat, wo_ref[...], preferred_element_type=F32)
        out_ref[rows] = mixed.astype(BF16).reshape(TILE_ROWS, grid_cols, feature)
        return carry

    lax.fori_loop(0, tile_rows, finish, 0)


def far_kernel(rels, tiles, phase, low, group, *refs):
    needed, totals, todo, todo_count, tile_of = refs[:5]
    refs = refs[5:]
    chunks = dict(zip(rels, refs[: len(rels)]))
    refs = refs[len(rels) :]
    mq_hbm, gain_ref, wk_ref, wv_ref = refs[:4]
    refs = refs[4:]
    late = phase == 1
    if late:
        near_hbm, early_hbm, tokens_ref, wo_ref, _, out_hbm = refs[:6]
        refs = refs[6:]
    else:
        acc_hbm = refs[0]
        refs = refs[1:]
    keys, values, wkv, raw, mq, acc, fetch_sems, mq_sems, acc_sems = refs[:9]
    if late:
        near, staged, near_sems, out_sems = refs[9:]
    tile_size, feature = raw.shape[1:]
    lanes = 2 * feature // HEADS
    count = totals[phase]
    slots = totals[2]
    gain = gain_ref[...].reshape(1, feature)

    def fetch(i, carry):
        rel, rank = split_by(needed[phase, i], tiles)
        for known, ref in chunks.items():
            @pl.when(rel == known)
            def _(ref=ref):
                pltpu.make_async_copy(ref.at[rank - low], raw.at[i], fetch_sems.at[i]).start()

        return carry

    def mq_copy(slot):
        return pltpu.make_async_copy(mq_hbm.at[slot], mq.at[slot], mq_sems.at[slot])

    def near_copy(slot):
        return pltpu.make_async_copy(near_hbm.at[slot], near.at[slot], near_sems.at[slot])

    def acc_copy(slot):
        if late:
            return pltpu.make_async_copy(early_hbm.at[slot], acc.at[slot], acc_sems.at[slot])
        return pltpu.make_async_copy(acc.at[slot], acc_hbm.at[slot], acc_sems.at[slot])

    def each_slot(work, when=None):
        def run(slot, carry):
            if when is None:
                work(slot)
            else:
                pl.when(when(slot))(lambda: work(slot))
            return carry

        lax.fori_loop(0, slots, run, 0)

    had_early = lambda slot: todo_count[0, slot] > 0
    active = lambda slot: todo_count[phase, slot] > 0
    lax.fori_loop(0, count, fetch, 0)
    each_slot(lambda slot: mq_copy(slot).start(), active)
    if late:
        each_slot(lambda slot: acc_copy(slot).start(), had_early)
        each_slot(lambda slot: near_copy(slot).start())
    wkv[:, :feature] = wk_ref[...]
    wkv[:, feature:] = wv_ref[...]

    def project(i, carry):
        def arrived(k, carry):
            pltpu.make_async_copy(chunks[0].at[0], raw.at[k], fetch_sems.at[k]).wait()
            return carry

        lax.fori_loop(group * i, jnp.minimum(group * (i + 1), count), arrived, 0)
        at = pl.ds(group * i, group)
        flat = raw[at].reshape(group * tile_size, feature).astype(F32)
        normed = normed_of(flat, gain)[0].astype(BF16)
        both = jnp.dot(normed, wkv[...], preferred_element_type=F32)
        keys[at] = unit(both[:, :feature]).astype(BF16).reshape(group, tile_size, feature)
        values[at] = both[:, feature:].astype(BF16).reshape(group, tile_size, feature)
        return carry

    lax.fori_loop(0, (count + group - 1) // group, project, 0)
    each_slot(lambda slot: mq_copy(slot).wait(), active)
    if late:
        each_slot(lambda slot: acc_copy(slot).wait(), had_early)
        each_slot(lambda slot: near_copy(slot).wait())

        def join(slot, carry):
            @pl.when(had_early(slot))
            def _():
                near[slot] += acc[slot]

            return carry

        lax.fori_loop(0, slots, join, 0)

    first = lax.broadcasted_iota(jnp.int32, (tile_size, lanes), 1) < lanes // 2
    zero = jnp.zeros((tile_size, lanes), BF16)
    ones = jnp.ones((tile_size, lanes), BF16)

    def attend(slot, carry):
        have = todo_count[phase, slot]

        def wide(width):
            picks = [todo[phase, slot, jnp.minimum(k, have - 1)] for k in range(width)]
            there = [jnp.where(k < have, 1.0, 0.0).astype(BF16) for k in range(width)]
            for p in range(feature // lanes):
                part = slice(p * lanes, (p + 1) * lanes)
                key = jnp.concatenate([keys[at, :, part] for at in picks], axis=0)
                value = jnp.concatenate(
                    [jnp.concatenate([values[at, :, part], ones], axis=1) * is_there
                     for at, is_there in zip(picks, there)], axis=0)
                q = mq[slot, :, part]
                stacked = jnp.concatenate([jnp.where(first, q, zero), jnp.where(first, zero, q)], axis=0)
                weights = jnp.exp2(contract_last(stacked, key)).astype(BF16)
                both = jnp.dot(weights, value, preferred_element_type=F32)
                num = jnp.where(first, both[:tile_size, :lanes], both[tile_size:, :lanes])
                den = jnp.where(first, both[:tile_size, lanes:], both[tile_size:, lanes:])
                if late:
                    near[slot, 0, :, part] += num
                    near[slot, 1, :, part] += den
                else:
                    acc[slot, 0, :, part] = num
                    acc[slot, 1, :, part] = den

        pl.when((have > 0) & (have <= 2))(lambda: wide(2))
        pl.when(have > 2)(lambda: wide(S_MAX))
        if not late:
            pl.when(have > 0)(lambda: acc_copy(slot).start())
        return carry

    lax.fori_loop(0, slots, attend, 0)
    if not late:
        each_slot(lambda slot: acc_copy(slot).wait(), active)
        return

    tile_cols = tokens_ref.shape[1] // TILE_COLS

    def place_of(slot):
        a, b = split_by(tile_of[slot], tile_cols)
        return pl.ds(a * TILE_ROWS, TILE_ROWS), pl.ds(pl.multiple_of(b * TILE_COLS, TILE_COLS), TILE_COLS)

    def out_copy(slot):
        return pltpu.make_async_copy(staged.at[slot], out_hbm.at[place_of(slot)], out_sems.at[slot])

    def finish(slot, carry):
        half = tile_size // 2
        sides = []
        for side in range(2):
            rows = slice(side * half, (side + 1) * half)
            sides.append((near[slot, 0, rows] / near[slot, 1, rows]).reshape(TILE_ROWS, SIDE, feature))
        attended = jnp.concatenate(sides, axis=1).reshape(tile_size, feature).astype(BF16)
        mixed = tokens_ref[place_of(slot)].reshape(tile_size, feature).astype(F32) + jnp.dot(
            attended, wo_ref[...], preferred_element_type=F32
        )
        staged[slot] = mixed.astype(BF16).reshape(TILE_ROWS, TILE_COLS, feature)
        out_copy(slot).start()
        return carry

    lax.fori_loop(0, slots, finish, 0)
    each_slot(lambda slot: out_copy(slot).wait())


def body(
    tokens,
    norm_gain,
    query_weight,
    key_weight,
    value_weight,
    out_weight,
    head_scale,
    counts,
    sources,
):
    grid_rows, grid_cols, feature = tokens.shape
    tile_rows = grid_rows // TILE_ROWS
    tile_cols = grid_cols // TILE_COLS
    tiles = tile_rows * tile_cols
    tile_size = TILE_ROWS * TILE_COLS
    keep = tiles - min(4, MASK_MOST)
    col_count = lax.axis_size("col")
    vmem = pl.BlockSpec(memory_space=pltpu.VMEM)
    smem = pl.BlockSpec(memory_space=pltpu.SMEM)
    hbm = pl.BlockSpec(memory_space=pl.ANY)

    free = jnp.repeat(jnp.repeat(counts == 0, TILE_ROWS, axis=0), TILE_COLS, axis=1)[..., None]
    mark = jnp.asarray(MARK, tokens.dtype)
    left = jnp.where(free[:, :RADIUS], tokens[:, :RADIUS], mark)
    right = jnp.where(free[:, -RADIUS:], tokens[:, -RADIUS:], mark)
    with jax.named_scope("halo_col"):
        before, after = pair_swap(left, right, "col")
    gap = jnp.full((grid_rows, GAP, feature), mark)
    tail = jnp.concatenate([after, gap, before], axis=1)
    upper = jnp.concatenate([jnp.where(free[:RADIUS], tokens[:RADIUS], mark), tail[:RADIUS]], axis=1)
    lower = jnp.concatenate([jnp.where(free[-RADIUS:], tokens[-RADIUS:], mark), tail[-RADIUS:]], axis=1)
    with jax.named_scope("halo_row"):
        top, bottom = pair_swap(upper, lower, "row")

    sizes = (keep - LATE_TILES, LATE_TILES)
    packed = pl.pallas_call(
        functools.partial(pack_kernel, tile_cols),
        out_shape=[jax.ShapeDtypeStruct((n, tile_size, feature), tokens.dtype) for n in sizes],
        in_specs=[smem, vmem],
        out_specs=[vmem] * 2,
        name="pack",
    )(counts, tokens)
    with jax.named_scope("spread_counts"):
        rel_counts = spread(counts, "col")
    with jax.named_scope("spread_early"):
        early = spread(packed[0], "col")
    with jax.named_scope("spread_late"):
        late = spread(packed[1], "col")

    rels = sorted(rel_counts)
    slots = MASK_MOST * S_MAX
    ints = lambda *shape: jax.ShapeDtypeStruct(shape, jnp.int32)
    plan = pl.pallas_call(
        functools.partial(plan_kernel, rels, tile_cols * col_count, sizes[0]),
        out_shape=[ints(2, slots), ints(3), ints(2, MASK_MOST, S_MAX), ints(2, MASK_MOST), ints(MASK_MOST + 1)],
        in_specs=[smem] * (2 + len(rels)),
        out_specs=[smem] * 5,
        scratch_shapes=[pltpu.SMEM((col_count * tiles,), jnp.int32)] * 2,
        name="plan",
    )(counts, sources, *[rel_counts[r] for r in rels])

    acc_shape = jax.ShapeDtypeStruct((MASK_MOST, 2, tile_size, feature), F32)
    padded = grid_rows + 2 * RADIUS
    lanes = 2 * feature // HEADS
    out, acc, mq = pl.pallas_call(
        near_kernel,
        out_shape=[
            jax.ShapeDtypeStruct(tokens.shape, tokens.dtype),
            jax.ShapeDtypeStruct((MASK_MOST + 1, 2, tile_size, feature), F32),
            jax.ShapeDtypeStruct((MASK_MOST + 1, tile_size, feature), BF16),
        ],
        in_specs=[smem] * 2 + [vmem] * 9,
        out_specs=[vmem] * 3,
        scratch_shapes=[
            pltpu.VMEM((2, padded, grid_cols, feature), BF16),
            pltpu.VMEM((2, padded, grid_cols, feature), BF16),
            pltpu.VMEM((2, padded, grid_cols, lanes), BF16),
            pltpu.VMEM((tile_rows, grid_cols // SIDE, TILE_ROWS * SIDE, feature), BF16),
            pltpu.VMEM(tokens.shape, BF16),
            pltpu.VMEM((feature, 2 * feature), BF16),
        ],
        cost_estimate=pl.CostEstimate(flops=20_000_000_000, bytes_accessed=20_000_000, transcendentals=3_000_000),
        name="near",
    )(head_scale, counts, tokens, tail, top, bottom, norm_gain, query_weight, key_weight, value_weight, out_weight)

    def far(phase, chunks):
        group = 2 if phase else 4
        args = [*plan, *[chunks[r] for r in rels], mq, norm_gain, key_weight, value_weight]
        specs = [smem] * 5 + [hbm] * (len(rels) + 1) + [vmem] * 3
        sems = lambda n: pltpu.SemaphoreType.DMA((n,))
        scratch = [
            pltpu.VMEM((slots + group, tile_size, feature), BF16),
            pltpu.VMEM((slots + group, tile_size, feature), BF16),
            pltpu.VMEM((feature, 2 * feature), BF16),
            pltpu.VMEM((slots + group, tile_size, feature), BF16),
            pltpu.VMEM((MASK_MOST, tile_size, feature), BF16),
            pltpu.VMEM(acc_shape.shape, F32),
            sems(slots),
            sems(MASK_MOST),
            sems(MASK_MOST),
        ]
        if phase:
            args += [acc, early_acc, tokens, out_weight, out]
            specs += [hbm, hbm, vmem, vmem, hbm]
            scratch += [
                pltpu.VMEM(acc_shape.shape, F32),
                pltpu.VMEM((MASK_MOST, TILE_ROWS, TILE_COLS, feature), BF16),
                sems(MASK_MOST),
                sems(MASK_MOST),
            ]
        return pl.pallas_call(
            functools.partial(far_kernel, rels, tiles, phase, sizes[0] if phase else 0, group),
            out_shape=jax.ShapeDtypeStruct(out.shape, out.dtype) if phase else acc_shape,
            in_specs=specs,
            out_specs=hbm,
            scratch_shapes=scratch,
            input_output_aliases={len(args) - 1: 0} if phase else {},
            cost_estimate=pl.CostEstimate(flops=5_000_000_000, bytes_accessed=10_000_000, transcendentals=1_000_000),
            name="far_late" if phase else "far_early",
        )(*args)

    early_acc = far(0, early)
    return far(1, late)


def solution(mesh):
    placed = (
        P(("slab", "row"), "col", None),
        P(),
        P(),
        P(),
        P(),
        P(),
        P(),
        P(("slab", "row"), "col"),
        P(("slab", "row"), "col", None),
    )
    return jax.shard_map(
        body, mesh=mesh, in_specs=placed, out_specs=P(("slab", "row"), "col", None), check_vma=False
    )
```

time: 111 us -> 90 us (0.81)
  the two profiles are of different devices: /device:TPU:8 before, /device:TPU:25 now
where the time goes in v2:
time: 90 us; the launch traced here: 89.1 us
  Pallas kernels  58.3 us (65%)
  waiting for transfers between devices  13.6 us (15%)
  starting transfers between devices  10 us (11%)
  other arithmetic  4.11 us (5%)
  local copies, waits for them, and re-layouts  2.91 us (3%)
    pallas_call x1, Pallas kernels, body(): pl.pallas_call(near_kernel, out_shape=[jax.ShapeDtypeStruct(tokens.shape,...  30.1 us
    pallas_call x2, Pallas kernels, far(): pl.pallas_call(functools.partial(far_kernel, rels, tiles, phase, sizes[0]...  22.5 us
    ppermute x9, waiting for transfers between devices, spread(): lax.ppermute(item, axis, pairs)  13.6 us
    ppermute x9, starting transfers between devices, spread(): lax.ppermute(item, axis, pairs)  3.94 us
    ppermute x2, starting transfers between devices, pair_swap(): two = lax.ppermute(jnp.where(even, low, high), axis, both(second))  3.7 us
    pallas_call x1, Pallas kernels, body(): pl.pallas_call(functools.partial(plan_kernel, rels, tile_cols * col_count...  2.86 us
    pallas_call x1, Pallas kernels, body(): pl.pallas_call(functools.partial(pack_kernel, tile_cols), out_shape=[jax....  2.81 us
    ppermute x2, starting transfers between devices, pair_swap(): one = lax.ppermute(jnp.where(even, high, low), axis, both(first))  2.38 us
  transfers between devices with their start and end apart: 13, of which 2 were waited for; matrix products, arithmetic and copies ran while one was open for 3% of the time, Pallas kernels for 54%

profile of v2, /device:TPU:25, one launch (start us, length us, event | category | flops | bytes accessed | tf_op | source)
XLA Modules:
  0.0 89.1 jit_solution(14877096346402193921)
XLA Ops:
  0.0 0.7 broadcast_compare_fusion
  0.7 0.1 copy.11
  0.8 0.1 broadcast_in_dim.66
  0.9 0.1 reshape.7
  1.0 0.1 copy.12
  1.1 0.1 copy.13
  1.2 1.2 %broadcast_select_fusion.3 = (bf16[32,3,384]{2,1,0:T(4,128)(2,1)S(1)}, bf16[32,3,384]{2,1,0:T(4,128)(2,1)S(1)}) fusion(pred[]{:T(512)S(6)} %eq.25, bf16[32,64,384]{2,1,0:T(8,128)(2,1)} %refs_15_.1, pred[32,3]{1,0:T(8,128)(4,1)S(1)} %copy.12, pred[32,3]{1,0:T(8,128)(4,1)S(1)} %copy.13), kind=kLoop, calls=%fused_computation.14 | loop fusion | flops 147456 | bytes 295105 | tf_op jit(solution)/shard_map/halo_col/jit(_where)/select_n | solution.py:33
  2.4 0.7 collective-permute-start.6
  3.2 0.0 copy-start.1
  3.2 3.0 %collective-permute-start.7 = (bf16[32,3,384]{2,1,0:T(4,128)(2,1)S(1)}, bf16[32,3,384]{2,1,0:T(4,128)(2,1)S(1)}, u32[]{:S(2)}, u32[]{:S(2)}) collective-permute-start(bf16[32,3,384]{2,1,0:T(4,128)(2,1)S(1)} %get-tuple-element.26), channel_id=1, source_target_pairs={{4,8},{8,4},{5,9},{9,5},{6,10},{10,6},{7,11},{11,7},{20,24},{24,20... | collective-permute-start | bytes 221192 | tf_op jit(solution)/shard_map/halo_col/ppermute | solution.py:34
  6.2 2.8 %pack.1 = (bf16[8,128,384]{2,1,0:T(8,128)(2,1)}, bf16[4,128,384]{2,1,0:T(8,128)(2,1)}) custom-call(s32[4,4]{1,0:T(4,128)} %counts_ref.5, bf16[32,64,384]{2,1,0:T(8,128)(2,1)} %refs_15_.1), custom_call_target="tpu_custom_call" | custom-call | tf_op jit(solution)/shard_map/pack/pallas_call | solution.py:465
  9.0 0.0 copy-start.5
  9.0 0.0 collective-permute-start.11
  9.0 0.1 fusion.1
  9.1 0.1 copy.14
  9.2 0.1 broadcast_in_dim.74
  9.3 0.1 broadcast_in_dim.75
  9.4 0.1 copy.15
  9.5 0.1 broadcast_in_dim.78
  9.6 0.1 broadcast_in_dim.79
  9.7 1.1 %slice_select_fusion.1 = (bf16[3,64,384]{2,1,0:T(8,128)(2,1)S(1)}, bf16[3,64,384]{2,1,0:T(8,128)(2,1)S(1)}) fusion(bf16[32,64,384]{2,1,0:T(8,128)(2,1)} %refs_15_.1, pred[3,64]{1,0:T(4,128)(4,1)S(1)} %broadcast_in_dim.75, pred[3,64]{1,0:T(4,128)(4,1)S(1)} %broadcast_in_dim.79), kind=kLoop, calls=%fused_computation.8 | loop fusion | flops 147456 | bytes 590208 | tf_op jit(solution)/shard_map/jit(_where)/select_n | solution.py:459
  10.8 0.1 pad.5.clone
  10.9 0.0 collective-permute-done.6
  10.9 0.0 collective-permute-done.7
  10.9 0.1 select_select_fusion.3
  11.0 0.1 pad_maximum_fusion.tail_ref
  11.1 0.0 copy-start
  11.1 0.1 broadcast_select_fusion
  11.2 0.7 collective-permute-start.8
  11.9 1.6 %collective-permute-start.9 = (bf16[3,72,384]{2,1,0:T(8,128)(2,1)S(1)}, bf16[3,72,384]{2,1,0:T(8,128)(2,1)S(1)}, u32[]{:S(2)}, u32[]{:S(2)}) collective-permute-start(bf16[3,72,384]{2,1,0:T(8,128)(2,1)S(1)} %get-tuple-element.31), channel_id=1, source_target_pairs={{0,1},{2,3},{1,0},{3,2},{4,5},{6,7},{5,4},{7,6},{8,9},{10,11},{9,8... | collective-permute-start | bytes 497672 | tf_op jit(solution)/shard_map/halo_row/ppermute | solution.py:33
  13.5 0.0 copy-done.1
  13.5 1.5 %collective-permute-start.1 = (s32[4,4]{1,0:T(4,128)S(1)}, s32[4,4]{1,0:T(4,128)S(1)}, u32[]{:S(2)}, u32[]{:S(2)}) collective-permute-start(s32[4,4]{1,0:T(4,128)S(1)} %copy-done.1), channel_id=1, source_target_pairs={{0,8},{4,12},{8,0},{12,4},{1,9},{5,13},{9,1},{13,5},{2,10},{6,14},... | collective-permute-start | bytes 200 | tf_op jit(solution)/shard_map/spread_counts/ppermute | solution.py:47
  15.0 0.2 collective-permute-start
  15.2 12.9 %collective-permute-done.1.refs_2_ = s32[4,4]{1,0:T(4,128)S(1)} collective-permute-done((s32[4,4]{1,0:T(4,128)S(1)}, s32[4,4]{1,0:T(4,128)S(1)}, u32[]{:S(2)}, u32[]{:S(2)}) %collective-permute-start.1) | collective-permute-done | bytes 96 | tf_op jit(solution)/shard_map/spread_counts/ppermute | solution.py:47
  28.2 0.3 collective-permute-start.2
  28.5 0.0 collective-permute-done.refs_1_
  28.5 0.0 copy-done.5
  28.5 0.2 collective-permute-start.10
  28.8 0.6 collective-permute-done.2.refs_3_
  29.4 0.8 collective-permute-start.4
  30.1 0.0 copy-done.2
  30.1 0.0 copy-done.3
  30.1 0.0 copy-done.4
  30.1 2.9 %plan.1 = (s32[2,32]{1,0:T(2,128)}, s32[3]{0:T(128)}, s32[2,8,4]{2,1,0:T(8,128)}, s32[2,8]{1,0:T(2,128)}, s32[9]{0:T(128)}) custom-call(s32[4,4]{1,0:T(4,128)} %counts_ref.5, s32[4,4,4]{2,1,0:T(4,128)} %sources_ref.1, s32[4,4]{1,0:T(4,128)} %counts_ref.5, s32[4,4]{1,0:T(4,128)} %copy-done.3, s32[4,4]{1,0:T(4,128)} %copy-done.2, s32[4,4]{1,0:T(4,128)} %copy-done.4), custom_call_target="tpu_custom_call" | custom-call | tf_op jit(solution)/shard_map/plan/pallas_call | solution.py:482
  33.0 0.0 collective-permute-done.8
  33.0 0.3 collective-permute-start.3
  33.3 0.0 collective-permute-done.9
  33.3 0.8 select_select_fusion
  34.1 0.0 collective-permute-done.11.refs_7_
  34.1 0.3 collective-permute-start.12
  34.4 0.0 copy-done
  34.4 30.1 %near.1 = (bf16[32,64,384]{2,1,0:T(8,128)(2,1)}, f32[9,2,128,384]{3,2,1,0:T(8,128)}, bf16[9,128,384]{2,1,0:T(8,128)(2,1)}) custom-call(f32[6]{0:T(128)} %scale_ref.1, s32[4,4]{1,0:T(4,128)} %counts_ref.5, bf16[32,64,384]{2,1,0:T(8,128)(2,1)} %refs_15_.1, bf16[32,8,384]{2,1,0:T(8,128)(2,1)} %copy-done, bf16[3,72,384]{2,1,0:T(8,128)(2,1)} %get-tuple-element.30.top_ref, ...), custom_call_target="tpu_custom_call" | custom-call | flops 20000000000 | bytes 20000000 | tf_op jit(solution)/shard_map/near/pallas_call | solution.py:494
  64.5 0.0 copy-done.6
  64.5 0.0 collective-permute-done.4.refs_7_
  64.5 0.3 collective-permute-start.5
  64.9 0.0 collective-permute-done.10.refs_6_
  64.9 0.0 collective-permute-done.12.refs_8_
  64.9 0.9 copy-done.7
  65.7 12.3 %far_early.1.refs_14_ = f32[8,2,128,384]{3,2,1,0:T(8,128)} custom-call(s32[2,32]{1,0:T(2,128)} %get-tuple-element.15.refs_0_, s32[3]{0:T(128)} %get-tuple-element.16.refs_1_, s32[2,8,4]{2,1,0:T(8,128)} %get-tuple-element.17.refs_2_, s32[2,8]{1,0:T(2,128)} %get-tuple-element.18.refs_3_, s32[9]{0:T(128)} %get-tuple-element.19.refs_4_, ...), custom_call_target="tpu_custom_call" | custom-call | flops 5000000000 | bytes 10000000 | tf_op jit(solution)/shard_map/far_early/pallas_call | solution.py:540
  78.1 0.0 collective-permute-done.3.refs_6_
  78.1 0.0 collective-permute-done.5.refs_8_
  78.1 0.0 copy-start.8
  78.1 0.8 copy-done.8
  78.9 10.2 %far_late.1 = bf16[32,64,384]{2,1,0:T(8,128)(2,1)} custom-call(s32[2,32]{1,0:T(2,128)} %get-tuple-element.15.refs_0_, s32[3]{0:T(128)} %get-tuple-element.16.refs_1_, s32[2,8,4]{2,1,0:T(8,128)} %get-tuple-element.17.refs_2_, s32[2,8]{1,0:T(2,128)} %get-tuple-element.18.refs_3_, s32[9]{0:T(128)} %get-tuple-element.19.refs_4_, ...), custom_call_target="tpu_custom_call", output_to_operand_aliasing={{}: (17, {})} | custom-call | flops 5000000000 | bytes 10000000 | tf_op jit(solution)/shard_map/far_late/pallas_call | solution.py:540
  (9 shorter events, 0.0 us)
Async XLA Ops:
  2.4 8.4 %collective-permute-start.6 = (bf16[32,3,384]{2,1,0:T(4,128)(2,1)S(1)}, bf16[32,3,384]{2,1,0:T(4,128)(2,1)S(1)}, u32[]{:S(2)}, u32[]{:S(2)}) collective-permute-start(bf16[32,3,384]{2,1,0:T(4,128)(2,1)S(1)} %get-tuple-element.25), channel_id=1, source_target_pairs={{0,4},{8,12},{4,0},{12,8},{1,5},{9,13},{5,1},{13,9},{2,6},{10,14},... | collective-permute-start | bytes 221192 | tf_op jit(solution)/shard_map/halo_col/ppermute | solution.py:33
  3.2 10.4 %copy-start.1 = (s32[4,4]{1,0:T(4,128)S(1)}, s32[4,4]{1,0:T(4,128)}, u32[]{:S(2)}) copy-start(s32[4,4]{1,0:T(4,128)} %counts_ref.5) | copy-start | bytes 196
  3.2 7.7 %collective-permute-start.7 = (bf16[32,3,384]{2,1,0:T(4,128)(2,1)S(1)}, bf16[32,3,384]{2,1,0:T(4,128)(2,1)S(1)}, u32[]{:S(2)}, u32[]{:S(2)}) collective-permute-start(bf16[32,3,384]{2,1,0:T(4,128)(2,1)S(1)} %get-tuple-element.26), channel_id=1, source_target_pairs={{4,8},{8,4},{5,9},{9,5},{6,10},{10,6},{7,11},{11,7},{20,24},{24,20... | collective-permute-start | bytes 221192 | tf_op jit(solution)/shard_map/halo_col/ppermute | solution.py:34
  9.0 19.5 %copy-start.5 = (bf16[8,128,384]{2,1,0:T(8,128)(2,1)S(1)}, bf16[8,128,384]{2,1,0:T(8,128)(2,1)}, u32[]{:S(2)}) copy-start(bf16[8,128,384]{2,1,0:T(8,128)(2,1)} %get-tuple-element.23.refs_5_) | copy-start | bytes 2359300
  9.0 25.1 %collective-permute-start.11 = (bf16[8,128,384]{2,1,0:T(8,128)(2,1)}, bf16[8,128,384]{2,1,0:T(8,128)(2,1)S(1)}, u32[]{:S(2)}, u32[]{:S(2)}) collective-permute-start(bf16[8,128,384]{2,1,0:T(8,128)(2,1)} %get-tuple-element.23.refs_5_), channel_id=1, source_target_pairs={{0,8},{4,12},{8,0},{12,4},{1,9},{5,13},{9,1},{13,5},{2,10},{6,14},... | collective-permute-start | bytes 2359304 | tf_op jit(solution)/shard_map/spread_early/ppermute | solution.py:47
  11.1 23.3 %copy-start = (bf16[32,8,384]{2,1,0:T(8,128)(2,1)}, bf16[32,8,384]{2,1,0:T(8,128)(2,1)S(1)}, u32[]{:S(2)}) copy-start(bf16[32,8,384]{2,1,0:T(8,128)(2,1)S(1)} %pad_maximum_fusion.tail_ref) | copy-start | bytes 589828
  11.2 21.8 %collective-permute-start.8 = (bf16[3,72,384]{2,1,0:T(8,128)(2,1)S(1)}, bf16[3,72,384]{2,1,0:T(8,128)(2,1)S(1)}, u32[]{:S(2)}, u32[]{:S(2)}) collective-permute-start(bf16[3,72,384]{2,1,0:T(8,128)(2,1)S(1)} %get-tuple-element.32), channel_id=1, source_target_pairs={{1,2},{2,1},{5,6},{6,5},{9,10},{10,9},{13,14},{14,13},{17,18},{18,... | collective-permute-start | bytes 497672 | tf_op jit(solution)/shard_map/halo_row/ppermute | solution.py:34
  11.9 21.4 %collective-permute-start.9 = (bf16[3,72,384]{2,1,0:T(8,128)(2,1)S(1)}, bf16[3,72,384]{2,1,0:T(8,128)(2,1)S(1)}, u32[]{:S(2)}, u32[]{:S(2)}) collective-permute-start(bf16[3,72,384]{2,1,0:T(8,128)(2,1)S(1)} %get-tuple-element.31), channel_id=1, source_target_pairs={{0,1},{2,3},{1,0},{3,2},{4,5},{6,7},{5,4},{7,6},{8,9},{10,11},{9,8... | collective-permute-start | bytes 497672 | tf_op jit(solution)/shard_map/halo_row/ppermute | solution.py:33
  13.5 14.7 %collective-permute-start.1 = (s32[4,4]{1,0:T(4,128)S(1)}, s32[4,4]{1,0:T(4,128)S(1)}, u32[]{:S(2)}, u32[]{:S(2)}) collective-permute-start(s32[4,4]{1,0:T(4,128)S(1)} %copy-done.1), channel_id=1, source_target_pairs={{0,8},{4,12},{8,0},{12,4},{1,9},{5,13},{9,1},{13,5},{2,10},{6,14},... | collective-permute-start | bytes 200 | tf_op jit(solution)/shard_map/spread_counts/ppermute | solution.py:47
  15.0 13.5 %collective-permute-start = (s32[4,4]{1,0:T(4,128)S(1)}, s32[4,4]{1,0:T(4,128)S(1)}, u32[]{:S(2)}, u32[]{:S(2)}) collective-permute-start(s32[4,4]{1,0:T(4,128)S(1)} %copy-done.1), channel_id=1, source_target_pairs={{0,4},{4,0},{8,12},{12,8},{1,5},{5,1},{9,13},{13,9},{2,6},{6,2},{1... | collective-permute-start | bytes 200 | tf_op jit(solution)/shard_map/spread_counts/ppermute | solution.py:47
  28.2 1.9 %copy-start.2 = (s32[4,4]{1,0:T(4,128)}, s32[4,4]{1,0:T(4,128)S(1)}, u32[]{:S(2)}) copy-start(s32[4,4]{1,0:T(4,128)S(1)} %collective-permute-done.1.refs_2_) | copy-start | bytes 196
  28.2 1.2 %collective-permute-start.2 = (s32[4,4]{1,0:T(4,128)S(1)}, s32[4,4]{1,0:T(4,128)S(1)}, u32[]{:S(2)}, u32[]{:S(2)}) collective-permute-start(s32[4,4]{1,0:T(4,128)S(1)} %collective-permute-done.1.refs_2_), channel_id=1, source_target_pairs={{0,4},{4,0},{8,12},{12,8},{1,5},{5,1},{9,13},{13,9},{2,6},{6,2},{1... | collective-permute-start | bytes 200 | tf_op jit(solution)/shard_map/spread_counts/ppermute | solution.py:47
  28.5 1.6 %copy-start.3 = (s32[4,4]{1,0:T(4,128)}, s32[4,4]{1,0:T(4,128)S(1)}, u32[]{:S(2)}) copy-start(s32[4,4]{1,0:T(4,128)S(1)} %collective-permute-done.refs_1_) | copy-start | bytes 196
  28.5 36.3 %collective-permute-start.10 = (bf16[8,128,384]{2,1,0:T(8,128)(2,1)S(1)}, bf16[8,128,384]{2,1,0:T(8,128)(2,1)S(1)}, u32[]{:S(2)}, u32[]{:S(2)}) collective-permute-start(bf16[8,128,384]{2,1,0:T(8,128)(2,1)S(1)} %copy-done.5), channel_id=1, source_target_pairs={{0,4},{4,0},{8,12},{12,8},{1,5},{5,1},{9,13},{13,9},{2,6},{6,2},{1... | collective-permute-start | bytes 2359304 | tf_op jit(solution)/shard_map/spread_early/ppermute | solution.py:47
  29.4 0.8 copy-start.4
  29.4 35.2 %collective-permute-start.4 = (bf16[4,128,384]{2,1,0:T(8,128)(2,1)}, bf16[4,128,384]{2,1,0:T(8,128)(2,1)}, u32[]{:S(2)}, u32[]{:S(2)}) collective-permute-start(bf16[4,128,384]{2,1,0:T(8,128)(2,1)} %get-tuple-element.20.refs_5_), channel_id=1, source_target_pairs={{0,8},{4,12},{8,0},{12,4},{1,9},{5,13},{9,1},{13,5},{2,10},{6,14},... | collective-permute-start | bytes 1179656 | tf_op jit(solution)/shard_map/spread_late/ppermute | solution.py:47
  33.0 45.1 %collective-permute-start.3 = (bf16[4,128,384]{2,1,0:T(8,128)(2,1)}, bf16[4,128,384]{2,1,0:T(8,128)(2,1)}, u32[]{:S(2)}, u32[]{:S(2)}) collective-permute-start(bf16[4,128,384]{2,1,0:T(8,128)(2,1)} %get-tuple-element.20.refs_5_), channel_id=1, source_target_pairs={{0,4},{4,0},{8,12},{12,8},{1,5},{5,1},{9,13},{13,9},{2,6},{6,2},{1... | collective-permute-start | bytes 1179656 | tf_op jit(solution)/shard_map/spread_late/ppermute | solution.py:47
  34.1 30.4 %copy-start.6 = (bf16[8,128,384]{2,1,0:T(8,128)(2,1)}, bf16[8,128,384]{2,1,0:T(8,128)(2,1)S(1)}, u32[]{:S(2)}) copy-start(bf16[8,128,384]{2,1,0:T(8,128)(2,1)S(1)} %collective-permute-done.11.refs_7_) | copy-start | bytes 2359300
  34.1 30.7 %collective-permute-start.12 = (bf16[8,128,384]{2,1,0:T(8,128)(2,1)S(1)}, bf16[8,128,384]{2,1,0:T(8,128)(2,1)}, u32[]{:S(2)}, u32[]{:S(2)}) collective-permute-start(bf16[8,128,384]{2,1,0:T(8,128)(2,1)S(1)} %collective-permute-done.11.refs_7_), channel_id=1, source_target_pairs={{0,4},{4,0},{8,12},{12,8},{1,5},{5,1},{9,13},{13,9},{2,6},{6,2},{1... | collective-permute-start | bytes 2359304 | tf_op jit(solution)/shard_map/spread_early/ppermute | solution.py:47
  64.5 13.5 %collective-permute-start.5 = (bf16[4,128,384]{2,1,0:T(8,128)(2,1)}, bf16[4,128,384]{2,1,0:T(8,128)(2,1)S(1)}, u32[]{:S(2)}, u32[]{:S(2)}) collective-permute-start(bf16[4,128,384]{2,1,0:T(8,128)(2,1)} %collective-permute-done.4.refs_7_), channel_id=1, source_target_pairs={{0,4},{4,0},{8,12},{12,8},{1,5},{5,1},{9,13},{13,9},{2,6},{6,2},{1... | collective-permute-start | bytes 1179656 | tf_op jit(solution)/shard_map/spread_late/ppermute | solution.py:47
  64.9 0.9 copy-start.7
  78.1 0.8 copy-start.8
